TPU v7x, 256 devices: a whole 4x4x8 slice. The times are simulated.
256 devices in a mesh: dp: 4 (over x), tensor: 64 (over y, z, core).
Axes of the slice: x: 4, y: 4, z: 8, core: 2. Of those that a mesh axis runs over, the one named last changes fastest.
Arguments:
- tokens_in: bfloat16 [512, 4096], P('dp', 'tensor'), may hold values from -6 to 6
- out_grad: bfloat16 [512, 4096], P('dp', 'tensor'), may hold values from -6 to 6
- gate_blocks: bfloat16 [2048, 128, 128], P('tensor'), may hold values from -0.125 to 0.125
- up_blocks: bfloat16 [2048, 128, 128], P('tensor'), may hold values from -0.125 to 0.125
- down_blocks: bfloat16 [2048, 128, 128], P('tensor'), may hold values from -0.0625 to 0.0625
- gate_up_index: int32 [64, 32, 2], replicated, may hold values from 0 to 127, as said below
- down_index: int32 [64, 32, 2], replicated, may hold values from 0 to 127, as said below
Outputs:
- output: bfloat16 [512, 4096], P('dp', 'tensor')
- in_grad: bfloat16 [512, 4096], P('dp', 'tensor')
- gate_grads: bfloat16 [2048, 128, 128], P('tensor', 'dp')
- up_grads: bfloat16 [2048, 128, 128], P('tensor', 'dp')
- down_grads: bfloat16 [2048, 128, 128], P('tensor', 'dp')
Inputs may be any that keep to these rules, and one draw needn't show every extreme that they name: `gate_up_index`: Model-width blocks lie in 0 to 31, hidden-unit blocks in 0 to 127. No block is listed twice. The owner of hidden-unit block j is index j // 2 of tensor. Of one index's 32 entries at most 1 name hidden-unit blocks of any one owner, and in every draw some owner has exactly 1 entries from every index; other owners get from none up to all indices. `down_index`: Hidden-unit blocks lie in 0 to 127, model-width blocks in 0 to 31. No block is listed twice. The owner of hidden-unit block j is index j // 2 of tensor. Of one index's 32 entries at most 1 name hidden-unit blocks of any one owner, and in every draw some owner has exactly 1 entries from every index; other owners get from none up to all indices.
All inputs are finite; a program needn't handle non-finite values.
Results may differ from a plain program's by a relative error of at most 0.022.
Values may be sent and summed in bfloat16 or wider, within the bound.
A program may use at most 128 MiB of HBM per device.

v0:
```python
import jax
import jax.numpy as jnp
from jax import lax
from jax.sharding import PartitionSpec as P

FB = 128


def routing(index_list, key_col, other_col, own_count, slot_cap, my_index):
    tensor_size = index_list.shape[0]
    held_count = index_list.shape[1]
    key_blocks = index_list[:, :, key_col]
    other_idx = index_list[:, :, other_col]
    owners = key_blocks // own_count
    local_idx = key_blocks % own_count
    block_order = jnp.arange(held_count)
    before = block_order[None, :] < block_order[:, None]
    same_owner = owners[:, :, None] == owners[:, None, :]
    slot_rank = jnp.sum(jnp.logical_and(same_owner, before[None]), axis=2)
    slot_all = owners * slot_cap + slot_rank
    matches = jnp.logical_and(
        (owners == my_index)[:, :, None],
        slot_rank[:, :, None] == jnp.arange(slot_cap)[None, None, :],
    )
    is_found = jnp.any(matches, axis=1)
    recv_local = jnp.where(
        is_found, jnp.sum(jnp.where(matches, local_idx[:, :, None], 0), axis=1), -1
    )
    recv_other = jnp.sum(jnp.where(matches, other_idx[:, :, None], 0), axis=1)
    mine_slot = lax.dynamic_index_in_dim(slot_all, my_index, 0, keepdims=False)
    return (
        mine_slot,
        recv_local.reshape(tensor_size * slot_cap),
        recv_other.reshape(tensor_size * slot_cap),
    )


def per_device(tokens_in, out_grad, gate_blocks, up_blocks, down_blocks, gate_up_index, down_index):
    block_size = gate_blocks.shape[1]
    held_count = gate_blocks.shape[0]
    tok_rows = tokens_in.shape[0]
    tensor_size = lax.axis_size("tensor")
    my_index = lax.axis_index("tensor")
    blocks_f = FB
    own_count = blocks_f // tensor_size
    slot_cap = 2 * held_count // tensor_size
    slot_total = tensor_size * slot_cap
    gu_slot, gu_local, gu_other = routing(gate_up_index, 1, 0, own_count, slot_cap, my_index)
    dn_slot, dn_local, dn_other = routing(down_index, 0, 1, own_count, slot_cap, my_index)
    gu_mine = lax.dynamic_index_in_dim(gate_up_index, my_index, 0, keepdims=False)
    dn_mine = lax.dynamic_index_in_dim(down_index, my_index, 0, keepdims=False)
    own_ids = jnp.arange(own_count)[None, :]
    gu_onehot = (gu_local[:, None] == own_ids).astype(jnp.float32)
    dn_onehot = (dn_local[:, None] == own_ids).astype(jnp.float32)
    paired = jnp.concatenate([gate_blocks, up_blocks], axis=2)
    x_whole = lax.all_gather(tokens_in, "tensor", axis=1, tiled=True)
    blocks_d = x_whole.shape[1] // block_size
    x_blocks = x_whole.reshape(tok_rows, blocks_d, block_size)
    x_sel = jnp.take(x_blocks, gu_mine[:, 0], axis=1)
    partials = jnp.einsum("rnk,nkf->rnf", x_sel, paired, preferred_element_type=jnp.float32)
    outgoing = (
        jnp.zeros((tok_rows, slot_total, 2 * block_size), jnp.float32).at[:, gu_slot].set(partials)
    )
    arrived = lax.all_to_all(
        outgoing.astype(jnp.bfloat16), "tensor", split_axis=1, concat_axis=1, tiled=True
    ).astype(outgoing.dtype)
    col_sums = jnp.einsum("rsf,sl->rlf", arrived, gu_onehot, precision=lax.Precision.HIGHEST)
    gate_sum = col_sums[:, :, :block_size]
    up_sum = col_sums[:, :, block_size:]
    gate_sig = jax.nn.sigmoid(gate_sum)
    gate_act = gate_sum * gate_sig
    hidden = (gate_act * up_sum).astype(jnp.bfloat16)
    grad_whole = lax.all_gather(out_grad, "tensor", axis=1, tiled=True)
    grad_blocks = grad_whole.reshape(tok_rows, blocks_d, block_size)
    hidden_all = lax.all_gather(
        hidden.reshape(tok_rows, own_count * block_size), "tensor", axis=1, tiled=True
    )
    h_sel = jnp.take(hidden_all.reshape(tok_rows, blocks_f, block_size), dn_mine[:, 0], axis=1)
    out_parts = jnp.einsum("rnk,nkf->rnf", h_sel, down_blocks, preferred_element_type=jnp.float32)
    d_onehot = (dn_mine[:, 1][:, None] == jnp.arange(blocks_d)[None, :]).astype(jnp.float32)
    out_dense = jnp.einsum("rnf,nd->rdf", out_parts, d_onehot, precision=lax.Precision.HIGHEST)
    dy_sel = jnp.take(grad_blocks, dn_mine[:, 1], axis=1)
    hid_parts = jnp.einsum("rnf,nkf->rnk", dy_sel, down_blocks, preferred_element_type=jnp.float32)
    outgoing_h = (
        jnp.zeros((tok_rows, slot_total, block_size), jnp.float32).at[:, dn_slot].set(hid_parts)
    )
    arrived_dh = lax.all_to_all(
        outgoing_h.astype(jnp.bfloat16), "tensor", split_axis=1, concat_axis=1, tiled=True
    ).astype(outgoing_h.dtype)
    hidden_grad = jnp.einsum("rsf,sl->rlf", arrived_dh, dn_onehot, precision=lax.Precision.HIGHEST)
    down_w_grad = jnp.einsum("rnk,rnf->nkf", h_sel, dy_sel, preferred_element_type=jnp.float32)
    output = lax.psum_scatter(
        out_dense.reshape(tok_rows, blocks_d * block_size),
        "tensor",
        scatter_dimension=1,
        tiled=True,
    ).astype(jnp.bfloat16)
    gate_grad = hidden_grad * up_sum * gate_sig * (1.0 + gate_sum * (1.0 - gate_sig))
    up_grad = hidden_grad * gate_act
    both_grads = jnp.concatenate(
        [gate_grad.astype(jnp.bfloat16), up_grad.astype(jnp.bfloat16)], axis=2
    )
    back_send = jnp.take(both_grads, jnp.maximum(gu_local, 0), axis=1)
    back_send = jnp.where((gu_local >= 0)[None, :, None], back_send, jnp.zeros_like(back_send))
    returned = lax.all_to_all(back_send, "tensor", split_axis=1, concat_axis=1, tiled=True)
    gu_sel = jnp.take(returned, gu_slot, axis=1)
    gate_w_grad = jnp.einsum(
        "rnk,rnf->nkf", x_sel, gu_sel[:, :, :block_size], preferred_element_type=jnp.float32
    )
    up_w_grad = jnp.einsum(
        "rnk,rnf->nkf", x_sel, gu_sel[:, :, block_size:], preferred_element_type=jnp.float32
    )
    in_parts = jnp.einsum("rnf,nkf->rnk", gu_sel, paired, preferred_element_type=jnp.float32)
    r_onehot = (gu_mine[:, 0][:, None] == jnp.arange(blocks_d)[None, :]).astype(jnp.float32)
    in_dense = jnp.einsum("rnk,nd->rdk", in_parts, r_onehot, precision=lax.Precision.HIGHEST)
    in_grad = lax.psum_scatter(
        in_dense.reshape(tok_rows, blocks_d * block_size), "tensor", scatter_dimension=1, tiled=True
    ).astype(jnp.bfloat16)
    summed = (
        lax.psum_scatter(
            gate_w_grad.astype(jnp.bfloat16), "dp", scatter_dimension=1, tiled=True
        ).astype(jnp.float32),
        lax.psum_scatter(
            up_w_grad.astype(jnp.bfloat16), "dp", scatter_dimension=1, tiled=True
        ).astype(jnp.float32),
        lax.psum_scatter(
            down_w_grad.astype(jnp.bfloat16), "dp", scatter_dimension=1, tiled=True
        ).astype(jnp.float32),
    )
    return (
        output,
        in_grad,
        summed[0].astype(jnp.bfloat16),
        summed[1].astype(jnp.bfloat16),
        summed[2].astype(jnp.bfloat16),
    )


def solution(mesh):
    in_specs = (
        P("dp", "tensor"),
        P("dp", "tensor"),
        P("tensor", None, None),
        P("tensor", None, None),
        P("tensor", None, None),
        P(),
        P(),
    )
    out_specs = (
        P("dp", "tensor"),
        P("dp", "tensor"),
        P("tensor", "dp", None),
        P("tensor", "dp", None),
        P("tensor", "dp", None),
    )
    return jax.shard_map(
        per_device, mesh=mesh, in_specs=in_specs, out_specs=out_specs, check_vma=False
    )
```

profile of v0, /device:TPU:1, one launch (start us, length us, event | category | flops | bytes accessed | tf_op | source)
XLA Modules:
  0.0 842.9 jit_solution(729895510610050165)
XLA Ops:
  11.3 80.1 %all-gather.8.cloned.1.call-done = bf16[128,4096]{0,1:T(8,128)(2,1)} async-done(((bf16[128,64]{0,1:T(8,128)(2,1)}), bf16[128,4096]{0,1:T(8,128)(2,1)}) %all-gather.8.cloned.1.call-update) | async-done | bytes 1048592 | tf_op jit(solution)/shard_map/all_gather | solution.py:73
  96.9 2.5 broadcast_in_dim.93
  99.3 5.4 scatter_fusion.1
  104.7 3.9 convert_element_type.53
  108.6 6.9 all-to-all-start.1
  119.3 80.5 %all-gather.4.cloned.1.call-done = bf16[128,4096]{0,1:T(8,128)(2,1)} async-done(((bf16[128,64]{0,1:T(8,128)(2,1)}), bf16[128,4096]{0,1:T(8,128)(2,1)}) %all-gather.4.cloned.1.call-update) | async-done | bytes 1048592 | tf_op jit(solution)/shard_map/all_gather | solution.py:56
  199.8 2.9 gather_fusion.3
  202.7 4.3 fusion.18
  207.1 4.2 broadcast_in_dim.88
  211.3 8.3 scatter_fusion
  219.6 6.0 convert_element_type.49
  225.6 6.9 all-to-all-start
  232.7 2.8 fusion.2
  235.5 92.9 %all-to-all-done = bf16[128,64,256]{2,0,1:T(8,128)(2,1)} async-done(((bf16[128,64,256]{2,0,1:T(8,128)(2,1)}), bf16[128,64,256]{2,0,1:T(8,128)(2,1)}, u32[]{:S(2)}, u32[]{:S(2)}) %all-to-all-start) | async-done | bytes 4194336 | tf_op jit(solution)/shard_map/all_to_all | solution.py:64
  328.4 4.5 fusion
  333.1 2.8 gather_fusion.1
  335.9 4.0 select_bitcast_fusion
  339.8 5.9 all-to-all-start.2
  346.7 107.3 %all-to-all-done.2 = bf16[128,64,256]{2,0,1:T(8,128)(2,1)} async-done(((bf16[128,64,256]{2,0,1:T(8,128)(2,1)}), bf16[128,64,256]{2,0,1:T(8,128)(2,1)}, u32[]{:S(2)}, u32[]{:S(2)}) %all-to-all-start.2) | async-done | bytes 4194336 | tf_op jit(solution)/shard_map/all_to_all | solution.py:105
  454.0 4.3 gather_fusion.2
  468.2 3.0 copy.144
  471.6 6.4 copy.131
  478.0 2.9 gather_fusion
  481.9 2.4 fusion.6
  487.9 2.7 convolution_convert_fusion.2
  490.7 2.7 convolution_convert_fusion.1
  493.5 3.2 convolution_convert_fusion
  496.7 106.8 %reduce-scatter.8.cloned.1.call-done = f32[128,64]{0,1:T(8,128)} async-done(((f32[128,4096]{0,1:T(8,128)}), f32[128,64]{0,1:T(8,128)}) %reduce-scatter.8.cloned.1.call-update) | async-done | bytes 32784 | tf_op jit(solution)/shard_map/reduce_scatter | solution.py:116
  604.8 142.1 %reduce-scatter.6.cloned.1.call-done = f32[128,64]{0,1:T(8,128)} async-done(((f32[128,4096]{0,1:T(8,128)}), f32[128,64]{0,1:T(8,128)}) %reduce-scatter.6.cloned.1.call-update) | async-done | bytes 32784 | tf_op jit(solution)/shard_map/reduce_scatter | solution.py:92
  748.2 29.7 %reduce-scatter.10.cloned.1.call-done = bf16[32,32,128]{2,1,0:T(8,128)(2,1)} async-done(((bf16[32,128,128]{2,1,0:T(8,128)(2,1)}), bf16[32,32,128]{2,1,0:T(8,128)(2,1)}) %reduce-scatter.10.cloned.1.call-update) | async-done | bytes 262160 | tf_op jit(solution)/shard_map/reduce_scatter | solution.py:120
  778.0 29.0 %reduce-scatter.12.cloned.1.call-done = bf16[32,32,128]{2,1,0:T(8,128)(2,1)} async-done(((bf16[32,128,128]{2,1,0:T(8,128)(2,1)}), bf16[32,32,128]{2,1,0:T(8,128)(2,1)}) %reduce-scatter.12.cloned.1.call-update) | async-done | bytes 262160 | tf_op jit(solution)/shard_map/reduce_scatter | solution.py:123
  807.0 29.1 %reduce-scatter.14.cloned.1.call-done = bf16[32,32,128]{2,1,0:T(8,128)(2,1)} async-done(((bf16[32,128,128]{2,1,0:T(8,128)(2,1)}), bf16[32,32,128]{2,1,0:T(8,128)(2,1)}) %reduce-scatter.14.cloned.1.call-update) | async-done | bytes 262160 | tf_op jit(solution)/shard_map/reduce_scatter | solution.py:126
  (75 shorter events, 32.0 us)
Async XLA Ops:
  7.2 87.6 %copy-start = (bf16[32,128,128]{2,1,0:T(8,128)(2,1)S(1)}, bf16[32,128,128]{2,1,0:T(8,128)(2,1)}, u32[]{:S(2)}) copy-start(bf16[32,128,128]{2,1,0:T(8,128)(2,1)} %param.13) | copy-start | bytes 3145732
  7.2 84.3 %all-gather.8.cloned.1.call-start = ((), (), s32[]{:S(2)}) async-start(), calls=%async_computation.11 | async-start | bytes 1064960 | tf_op jit(solution)/shard_map/all_gather | solution.py:73
  108.6 117.0 %all-to-all-start.1 = ((bf16[128,64,128]{2,0,1:T(8,128)(2,1)}), bf16[128,64,128]{2,0,1:T(8,128)(2,1)}, u32[]{:S(2)}, u32[]{:S(2)}) async-start(bf16[128,64,128]{2,0,1:T(8,128)(2,1)} %convert_element_type.53), calls=%async_computation.2 | async-start | bytes 4194304 | tf_op jit(solution)/shard_map/all_to_all | solution.py:87
  115.5 84.3 %all-gather.4.cloned.1.call-start = ((), (), s32[]{:S(2)}) async-start(), calls=%async_computation.8 | async-start | bytes 1064960 | tf_op jit(solution)/shard_map/all_gather | solution.py:56
  225.6 102.8 %all-to-all-start = ((bf16[128,64,256]{2,0,1:T(8,128)(2,1)}), bf16[128,64,256]{2,0,1:T(8,128)(2,1)}, u32[]{:S(2)}, u32[]{:S(2)}) async-start(bf16[128,64,256]{2,0,1:T(8,128)(2,1)} %convert_element_type.49), calls=%async_computation | async-start | bytes 8388608 | tf_op jit(solution)/shard_map/all_to_all | solution.py:64
  339.8 114.1 %all-to-all-start.2 = ((bf16[128,64,256]{2,0,1:T(8,128)(2,1)}), bf16[128,64,256]{2,0,1:T(8,128)(2,1)}, u32[]{:S(2)}, u32[]{:S(2)}) async-start(bf16[128,64,256]{2,0,1:T(8,128)(2,1)} %select_bitcast_fusion), calls=%async_computation.3 | async-start | bytes 8388608 | tf_op jit(solution)/shard_map/all_to_all | solution.py:105
  345.8 125.8 %all-gather.6.cloned.1.call-start = ((), (), s32[]{:S(2)}) async-start(), calls=%async_computation.9 | async-start | bytes 4259840 | tf_op jit(solution)/shard_map/all_gather | solution.py:75
  346.6 256.8 %reduce-scatter.8.cloned.1.call-start = ((), (), s32[]{:S(2)}) async-start(), calls=%async_computation.12 | async-start | bytes 2129920 | tf_op jit(solution)/shard_map/reduce_scatter | solution.py:116
  460.1 1.3 copy-start.1
  471.2 275.6 %reduce-scatter.6.cloned.1.call-start = ((), (), s32[]{:S(2)}) async-start(), calls=%async_computation.10 | async-start | bytes 2129920 | tf_op jit(solution)/shard_map/reduce_scatter | solution.py:92
  480.9 1.0 copy-start.3
  486.3 1.6 copy-start.2
  486.3 291.7 %reduce-scatter.10.cloned.1.call-start = ((), (), s32[]{:S(2)}) async-start(), calls=%async_computation.13 | async-start | bytes 1310720 | tf_op jit(solution)/shard_map/reduce_scatter | solution.py:120
  490.6 316.4 %reduce-scatter.12.cloned.1.call-start = ((), (), s32[]{:S(2)}) async-start(), calls=%async_computation.14 | async-start | bytes 1310720 | tf_op jit(solution)/shard_map/reduce_scatter | solution.py:123
  493.4 342.6 %reduce-scatter.14.cloned.1.call-start = ((), (), s32[]{:S(2)}) async-start(), calls=%async_computation.15 | async-start | bytes 1310720 | tf_op jit(solution)/shard_map/reduce_scatter | solution.py:126
Sparse Core Ops, SparseCore 0:
  10.8 80.6 all-gather.7
  119.1 80.6 all-gather.3
  350.0 100.1 all-gather.5
  471.4 132.0 reduce-scatter.7
  607.9 138.9 reduce-scatter.5
  749.9 28.0 reduce-scatter.9
  781.2 25.6 reduce-scatter.11
  810.1 25.8 reduce-scatter.13
where the time goes:
time: 845 us; the launch traced here: 843 us
  waiting for transfers between devices  699 us (83%)
  local copies, waits for them, and re-layouts  60 us (7%)
  matrix products  29.8 us (4%)
  starting transfers between devices  20.2 us (2%)
  other arithmetic  19.5 us (2%)
  between operations  14.4 us (2%)
    reduce_scatter x1, waiting for transfers between devices, per_device(): lax.psum_scatter(out_dense.reshape(tok_rows, blocks_d * block_size), 'ten...  142 us
    all_to_all x1, waiting for transfers between devices, per_device(): lax.all_to_all(back_send, 'tensor', split_axis=1, concat_axis=1, tiled=True)  107 us
    reduce_scatter x1, waiting for transfers between devices, per_device(): lax.psum_scatter(in_dense.reshape(tok_rows, blocks_d * block_size), 'tens...  107 us
    all_to_all x1, waiting for transfers between devices, per_device(): lax.all_to_all(outgoing.astype(jnp.bfloat16), 'tensor', split_axis=1, con...  92.9 us
    all_gather x1, waiting for transfers between devices, per_device(): x_whole = lax.all_gather(tokens_in, 'tensor', axis=1, tiled=True)  80.5 us
    all_gather x1, waiting for transfers between devices, per_device(): grad_whole = lax.all_gather(out_grad, 'tensor', axis=1, tiled=True)  80.1 us
    reduce_scatter x1, waiting for transfers between devices, per_device(): lax.psum_scatter(gate_w_grad.astype(jnp.bfloat16), 'dp', scatter_dimensio...  29.7 us
    reduce_scatter x1, waiting for transfers between devices, per_device(): lax.psum_scatter(down_w_grad.astype(jnp.bfloat16), 'dp', scatter_dimensio...  29.1 us
  transfers between devices with their start and end apart: 11, of which 9 were waited for; matrix products, arithmetic and copies ran while one was open for 9% of the time, Pallas kernels for 0%

commit v1 on v0

v1 whole, which is shorter than its diff:
```python
import functools

import jax
import jax.numpy as jnp
from jax import lax
from jax.experimental import pallas as pl
from jax.experimental.pallas import tpu as pltpu
from jax.sharding import PartitionSpec as P

MESH = pl.DeviceIdType.MESH
BF = jnp.bfloat16
F32 = jnp.float32


def route_tables(lists, own, width_blocks, me):
    key = jnp.stack([k for k, _ in lists])
    other = jnp.stack([o for _, o in lists])
    nt, ne = key.shape[1:]
    owner = key // own
    cell = (key % own) * width_blocks + other
    my_owner = lax.dynamic_index_in_dim(owner, me, 1, keepdims=False)
    hit = my_owner[:, None, :] == jnp.arange(nt)[None, :, None]
    send = jnp.min(jnp.where(hit, jnp.arange(ne)[None, None, :], ne), axis=2)
    ret = jnp.max(jnp.where(owner == me, cell, -1), axis=2)
    match = ret[:, None, :] == jnp.arange(own * width_blocks)[None, :, None]
    source = jnp.min(jnp.where(match, jnp.arange(nt)[None, None, :], nt), axis=2)
    table = jnp.concatenate([send, source, jnp.maximum(ret, 0), my_owner], axis=1)
    return table.astype(jnp.int32).reshape(-1)


def kernel(
    cfg,
    idx,
    x_ref,
    dy_ref,
    gate_hbm,
    up_hbm,
    down_hbm,
    out_ref,
    in_ref,
    gg_ref,
    ug_ref,
    dg_ref,
    gu_in,
    dn_in,
    dn_t,
    xs,
    ws_gu,
    wr_gu,
    ws_dn,
    wr_dn,
    xall,
    wd,
    part,
    psum_in,
    hid,
    oall,
    c_in,
    tsum,
    y_in,
    usum,
    z_in,
    vsum,
    f_in,
    gc,
    gd,
    gs_gu,
    gr_gu,
    gs_dn,
    gr_dn,
    zl,
    zs,
    zr,
    load_sem,
    dpx_s,
    dpx_r,
    zg_s,
    zg_r,
    yg_s,
    yg_r,
    cg_s,
    cg_r,
    wdn_s,
    wdn_r,
    wgu_s,
    wgu_r,
    ph_s,
    ph_r,
    pg_s,
    pg_r,
    h_s,
    h_r,
    co_s,
    co_r,
    yo_s,
    yo_r,
    zo_s,
    zo_r,
    fo_s,
    fo_r,
    gdn_s,
    gdn_r,
    ggu_s,
    ggu_r,
    zx_s,
    zx_r,
):
    nx, ny, nz, ne, own, db = cfg
    nt = ny * nz * 2
    npl = ny * nz
    bs = 128
    tk = 128
    rr = bs // nx
    dpc = nx // 2
    fown = own * bs
    cells = own * db
    stride = nt + cells + nt + ne
    d = lax.axis_index("dp")
    t = lax.axis_index("tensor")
    c = t % 2
    chip = t // 2
    y = chip // nz
    z = chip % nz

    def dev(dd, tt):
        return (dd, tt)

    def rcopy(src, dst, ssem, rsem, dd, tt):
        return pltpu.make_async_remote_copy(
            src_ref=src,
            dst_ref=dst,
            send_sem=ssem,
            recv_sem=rsem,
            device_id=dev(dd, tt),
            device_id_type=MESH,
        )

    barrier = pltpu.get_barrier_semaphore()

    @pl.loop(1, nt)
    def _(i):
        pl.semaphore_signal(
            barrier, inc=1, device_id=dev(d, lax.rem(t + i, nt)), device_id_type=MESH
        )

    for k in range(1, nx):
        for cc in range(2):
            pl.semaphore_signal(
                barrier,
                inc=1,
                device_id=dev(lax.rem(d + k, nx), chip * 2 + cc),
                device_id_type=MESH,
            )

    rows = pl.ds(pl.multiple_of(d * rr, rr), rr)
    loads = [
        pltpu.make_async_copy(gate_hbm.at[:, rows, :], gu_in.at[0, pl.ds(0, ne)], load_sem.at[0]),
        pltpu.make_async_copy(up_hbm.at[:, rows, :], gu_in.at[1, pl.ds(0, ne)], load_sem.at[1]),
        pltpu.make_async_copy(down_hbm, dn_in, load_sem.at[2]),
    ]
    for cp in loads:
        cp.start()

    half = x_ref.shape[1]
    eye = (
        lax.broadcasted_iota(jnp.int32, (half, half), 0)
        == lax.broadcasted_iota(jnp.int32, (half, half), 1)
    ).astype(F32).astype(BF)
    nt_dims = (((1,), (1,)), ((), ()))
    for a, ref in enumerate((x_ref, dy_ref)):
        xt = lax.dot_general(eye, ref[...], nt_dims, preferred_element_type=F32)
        xs[a] = xt.astype(BF).reshape(dpc, rr, tk)

    zero_rows = jnp.zeros((rr, bs), BF)
    gu_in[0, ne] = zero_rows
    gu_in[1, ne] = zero_rows
    dn_t[ne] = zero_rows
    wr_gu[nt, 0] = zero_rows
    wr_gu[nt, 1] = zero_rows
    wr_dn[nt] = zero_rows

    loads[2].wait()
    pick = (
        lax.broadcasted_iota(jnp.int32, (rr, bs), 1)
        == lax.broadcasted_iota(jnp.int32, (rr, bs), 0) + d * rr
    ).astype(F32).astype(BF)

    @pl.loop(0, ne)
    def _(e):
        dn_t[e] = lax.dot_general(
            pick, dn_in[e], nt_dims, preferred_element_type=F32
        ).astype(BF)

    @pl.loop(0, nt)
    def _(s):
        ws_dn[s] = dn_t[idx[stride + s]]

    wr_dn[t] = ws_dn[t]
    loads[0].wait()
    loads[1].wait()

    @pl.loop(0, nt)
    def _(s):
        e = idx[s]
        ws_gu[s, 0] = gu_in[0, e]
        ws_gu[s, 1] = gu_in[1, e]

    wr_gu[t] = ws_gu[t]

    pl.semaphore_wait(barrier, nt - 1 + 2 * (nx - 1))

    def dpx(a, j, go):
        dst_d = c * dpc + j
        is_me = jnp.logical_and(dst_d == d, c == a)

        @pl.when(jnp.logical_not(is_me))
        def _():
            go(
                rcopy(
                    xs.at[a, j],
                    xall.at[a, chip, :, pl.ds(pl.multiple_of(d * tk, tk), tk)],
                    dpx_s.at[a, j],
                    dpx_r.at[d],
                    dst_d,
                    chip * 2 + a,
                )
            )

    for a in range(2):
        for j in range(dpc):
            dpx(a, j, lambda cp: cp.start())

    @pl.when(d // dpc == c)
    def _():
        xall[c, chip, :, pl.ds(pl.multiple_of(d * tk, tk), tk)] = xs[c, d % dpc]

    def a2a(src, dst, ssem, rsem, lo, hi):
        @pl.loop(lo, hi)
        def _(i):
            to = lax.rem(t + i, nt)
            rcopy(src.at[to], dst.at[t], ssem, rsem, d, to).start()

    def a2a_wait(src, dst, ssem, rsem, what):
        cp = rcopy(
            src.at[pl.ds(0, nt - 1)], dst.at[pl.ds(0, nt - 1)], ssem, rsem, d, lax.rem(t + 1, nt)
        )
        if what == "send":
            cp.wait_send()
        else:
            cp.wait_recv()

    a2a(ws_dn, wr_dn, wdn_s, wdn_r, 1, nt)

    for q in range(nx):

        @pl.when(jnp.logical_not(jnp.logical_and(q == d, d // dpc == c)))
        def _():
            rcopy(
                xs.at[0, 0],
                xall.at[c, chip, :, pl.ds(q * tk, tk)],
                dpx_s.at[0, 0],
                dpx_r.at[q],
                d,
                lax.rem(t + 1, nt),
            ).wait_recv()

    def zg(k):
        zz = lax.rem(z + k, nz)
        return rcopy(
            xall.at[c, chip],
            xall.at[c, chip],
            zg_s.at[k],
            zg_r.at[k],
            d,
            (y * nz + zz) * 2 + c,
        )

    for k in range(1, nz):
        zg(k).start()

    mid = nt // 2
    a2a(ws_gu, wr_gu, wgu_s, wgu_r, 1, mid)
    for k in range(1, nz):
        src_z = lax.rem(z - k + nz, nz)
        rcopy(
            xall.at[c, chip],
            xall.at[c, y * nz + src_z],
            zg_s.at[k],
            zg_r.at[k],
            d,
            lax.rem(t + 1, nt),
        ).wait_recv()

    def row_of(yy):
        return pl.ds(yy * nz, nz)

    for k in range(1, ny):
        yy = lax.rem(y + k, ny)
        rcopy(
            xall.at[c, row_of(y)],
            xall.at[c, row_of(y)],
            yg_s.at[k],
            yg_r.at[k],
            d,
            (yy * nz + z) * 2 + c,
        ).start()

    def to_core(k):
        yy = lax.rem(y - k + ny, ny)
        return rcopy(
            xall.at[c, row_of(yy)],
            xall.at[c, row_of(yy)],
            cg_s.at[k],
            cg_r.at[k],
            d,
            chip * 2 + 1 - c,
        )

    to_core(0).start()
    a2a(ws_gu, wr_gu, wgu_s, wgu_r, mid, nt)
    for k in range(1, ny):
        yy = lax.rem(y - k + ny, ny)
        rcopy(
            xall.at[c, row_of(y)],
            xall.at[c, row_of(yy)],
            yg_s.at[k],
            yg_r.at[k],
            d,
            lax.rem(t + 1, nt),
        ).wait_recv()
        to_core(k).start()
    for k in range(ny):
        yy = lax.rem(y - k + ny, ny)
        rcopy(
            xall.at[c, row_of(yy)],
            xall.at[1 - c, row_of(yy)],
            cg_s.at[k],
            cg_r.at[k],
            d,
            chip * 2 + 1 - c,
        ).wait_recv()

    a2a_wait(ws_dn, wr_dn, wdn_s, wdn_r, "recv")

    @pl.loop(0, db)
    def _(a):
        for jl in range(own):
            s = idx[stride + nt + jl * db + a]
            wd[a, :, pl.ds(2 * fown + jl * bs, bs)] = wr_dn[s]

    tn_dims = (((0,), (0,)), ((), ()))
    kall = db * rr
    tok = nx * tk

    def partials(lo, hi, arr):
        @pl.loop(lo, hi)
        def _(f):
            cols = pl.ds(pl.multiple_of(f * bs, bs), bs)
            lhs = wd[:, :, cols].reshape(kall, bs)
            rhs = xall[arr].reshape(kall, tok)
            res = lax.dot_general(lhs, rhs, tn_dims, preferred_element_type=F32)
            part[pl.ds(pl.multiple_of(f * bs, bs), bs), :] = res.astype(BF)

    def dp_out(lo, size, k, ssem, rsem):
        dd = lax.rem(d + k, nx)
        return rcopy(
            part.at[pl.ds(lo, size), pl.ds(pl.multiple_of(dd * tk, tk), tk)],
            psum_in.at[k, pl.ds(lo, size), :],
            ssem.at[k],
            rsem.at[k],
            dd,
            t,
        )

    partials(2 * own, 3 * own, 1)
    for k in range(1, nx):
        dp_out(2 * fown, fown, k, ph_s, ph_r).start()

    a2a_wait(ws_gu, wr_gu, wgu_s, wgu_r, "recv")

    @pl.loop(0, db)
    def _(a):
        for jl in range(own):
            s = idx[nt + jl * db + a]
            wd[a, :, pl.ds(jl * bs, bs)] = wr_gu[s, 0]
            wd[a, :, pl.ds(fown + jl * bs, bs)] = wr_gu[s, 1]

    partials(0, 2 * own, 0)
    for k in range(1, nx):
        dp_out(0, 2 * fown, k, pg_s, pg_r).start()
    for k in range(1, nx):
        dp_out(2 * fown, fown, k, ph_s, ph_r).wait_recv()
        dp_out(0, 2 * fown, k, pg_s, pg_r).wait_recv()

    my_tok = pl.ds(pl.multiple_of(d * tk, tk), tk)

    @pl.loop(0, own)
    def _(j):
        def total(base):
            r = pl.ds(pl.multiple_of(base + j * bs, bs), bs)
            acc = part[r, my_tok].astype(F32)
            for k in range(1, nx):
                acc += psum_in[k, r, :].astype(F32)
            return acc

        gate = total(0)
        up = total(fown)
        hg = total(2 * fown)
        sig = 1.0 / (1.0 + jnp.exp(-gate))
        act = gate * sig
        hid[pl.ds(pl.multiple_of(2 * fown + j * bs, bs), bs), my_tok] = (act * up).astype(BF)
        hid[pl.ds(pl.multiple_of(j * bs, bs), bs), my_tok] = (
            hg * up * sig * (1.0 + gate * (1.0 - sig))
        ).astype(BF)
        hid[pl.ds(pl.multiple_of(fown + j * bs, bs), bs), my_tok] = (hg * act).astype(BF)

    for k in range(1, nx):
        rcopy(
            hid.at[:, my_tok], hid.at[:, my_tok], h_s.at[k], h_r.at[k], lax.rem(d + k, nx), t
        ).start()
    for k in range(1, nx):
        src = lax.rem(d - k + nx, nx)
        rcopy(
            hid.at[:, my_tok],
            hid.at[:, pl.ds(pl.multiple_of(src * tk, tk), tk)],
            h_s.at[k],
            h_r.at[k],
            src,
            t,
        ).wait_recv()

    mt = 256 // rr

    @pl.loop(0, db // mt)
    def _(i):
        a0 = i * mt
        arows = pl.ds(a0, mt)
        for dst, lo, size in ((0, 2 * fown, fown), (1, 0, 2 * fown)):
            lhs = wd[arows, :, pl.ds(lo, size)].reshape(mt * rr, size)
            res = jnp.dot(lhs, hid[pl.ds(lo, size), :], preferred_element_type=F32)
            oall[dst, arows] = res.astype(BF).reshape(mt, rr, tok)

    other = chip * 2 + 1 - c
    core_out = rcopy(oall.at[1 - c], c_in, co_s, co_r, d, other)
    core_out.start()

    def grads(arr, lo, size):
        def body(i, store):
            lhs = xall[arr, pl.ds(i * mt, mt)].reshape(mt * rr, tok)
            res = lax.dot_general(
                lhs, hid[pl.ds(lo, size), :], nt_dims, preferred_element_type=F32
            )
            store(i * mt, res.astype(BF))

        return body

    def store_dn(a0, res):
        for jl in range(own):
            gd[pl.ds(jl * db + a0, mt)] = res[:, jl * bs : (jl + 1) * bs].reshape(mt, rr, bs)

    def store_gu(a0, res):
        for h in range(2):
            for jl in range(own):
                lo = h * fown + jl * bs
                gc[pl.ds(jl * db + a0, mt), h] = res[:, lo : lo + bs].reshape(mt, rr, bs)

    @pl.loop(0, db // mt)
    def _(i):
        grads(1, 2 * fown, fown)(i, store_dn)

    @pl.loop(0, nt)
    def _(s):
        gs_dn[s] = gd[idx[stride + nt + cells + s]]

    gr_dn[t] = gs_dn[t]
    a2a(gs_dn, gr_dn, gdn_s, gdn_r, 1, nt)

    @pl.loop(0, db // mt)
    def _(i):
        grads(0, 0, 2 * fown)(i, store_gu)

    @pl.loop(0, nt)
    def _(s):
        gs_gu[s] = gc[idx[nt + cells + s]]

    gr_gu[t] = gs_gu[t]

    core_out.wait_recv()

    @pl.loop(0, npl)
    def _(p):
        tsum[p] = (oall[c, p].astype(F32) + c_in[p].astype(F32)).astype(BF)

    for k in range(1, ny):
        yy = lax.rem(y + k, ny)
        rcopy(
            tsum.at[row_of(yy)], y_in.at[k], yo_s.at[k], yo_r.at[k], d, (yy * nz + z) * 2 + c
        ).start()
    a2a(gs_gu, gr_gu, ggu_s, ggu_r, 1, nt)
    for k in range(1, ny):
        rcopy(tsum.at[row_of(y)], y_in.at[k], yo_s.at[k], yo_r.at[k], d, other).wait_recv()

    @pl.loop(0, nz)
    def _(p):
        acc = tsum[y * nz + p].astype(F32)
        for k in range(1, ny):
            acc += y_in[k, p].astype(F32)
        usum[p] = acc.astype(BF)

    for k in range(1, nz):
        zz = lax.rem(z + k, nz)
        rcopy(
            usum.at[zz], z_in.at[k], zo_s.at[k], zo_r.at[k], d, (y * nz + zz) * 2 + c
        ).start()

    a2a_wait(gs_dn, gr_dn, gdn_s, gdn_r, "recv")
    groups = ne // nx

    @pl.loop(0, groups)
    def _(g):
        for p in range(nx):
            o = idx[stride + nt + cells + nt + g * nx + p]
            zl[g, :, pl.ds(p * bs, bs)] = gr_dn[o]

    lane = lax.broadcasted_iota(jnp.int32, (nx * bs, bs), 0)
    col = lax.broadcasted_iota(jnp.int32, (nx * bs, bs), 1)
    for dd in range(nx):
        want = (col // rr) * bs + dd * rr + col % rr
        perm = (lane == want).astype(F32).astype(BF)
        moved = jnp.dot(zl[...].reshape(groups * rr, nx * bs), perm, preferred_element_type=F32)
        zs[dd] = moved.astype(BF).reshape(groups, rr, bs)
    zr[d] = zs[d]
    for k in range(1, nx):
        dd = lax.rem(d + k, nx)
        rcopy(zs.at[dd], zr.at[d], zx_s.at[k], zx_r.at[k], dd, t).start()

    for k in range(1, nz):
        rcopy(usum.at[z], z_in.at[k], zo_s.at[k], zo_r.at[k], d, other).wait_recv()
    acc = usum[z].astype(F32)
    for k in range(1, nz):
        acc += z_in[k].astype(F32)
    vsum[...] = acc.astype(BF)

    fcore = chip * 2 + d // dpc

    def is_self(q):
        return jnp.logical_and(q == d, d // dpc == c)

    for q in range(nx):

        @pl.when(jnp.logical_not(is_self(q)))
        def _():
            rcopy(
                vsum.at[:, pl.ds(q * tk, tk)],
                f_in.at[c, d % dpc],
                fo_s.at[q],
                fo_r.at[c, d % dpc],
                q,
                fcore,
            ).start()

    @pl.when(d // dpc == c)
    def _():
        f_in[c, d % dpc] = vsum[:, my_tok]

    for k in range(1, nx):
        src = lax.rem(d - k + nx, nx)
        rcopy(zs.at[0], zr.at[src], zx_s.at[k], zx_r.at[k], src, t).wait_recv()
    eye_b = (
        lax.broadcasted_iota(jnp.int32, (bs, bs), 0) == lax.broadcasted_iota(jnp.int32, (bs, bs), 1)
    ).astype(F32).astype(BF)

    @pl.loop(0, groups)
    def _(g):
        block = zr[:, g].reshape(nx * rr, bs)
        flip = lax.dot_general(block, eye_b, tn_dims, preferred_element_type=F32)
        dg_ref[pl.ds(g * nx, nx)] = flip.astype(BF).reshape(nx, rr, bs)

    for a in range(2):
        for j in range(dpc):
            src_d = c * dpc + j
            own_piece = jnp.logical_and(src_d == d, a == c)

            @pl.when(jnp.logical_not(own_piece))
            def _():
                rcopy(
                    vsum.at[:, pl.ds(0, tk)],
                    f_in.at[a, j],
                    fo_s.at[0],
                    fo_r.at[a, j],
                    src_d,
                    other,
                ).wait_recv()

    for a, ref in enumerate((out_ref, in_ref)):
        block = f_in[a].reshape(half, tk)
        ref[...] = lax.dot_general(
            eye_b, block, nt_dims, preferred_element_type=F32
        ).astype(BF)

    a2a_wait(gs_gu, gr_gu, ggu_s, ggu_r, "recv")

    @pl.loop(0, ne)
    def _(e):
        o = idx[nt + cells + nt + e]
        gg_ref[e] = gr_gu[o, 0]
        ug_ref[e] = gr_gu[o, 1]

    for a in range(2):
        for j in range(dpc):
            dpx(a, j, lambda cp: cp.wait_send())
    a2a_wait(ws_dn, wr_dn, wdn_s, wdn_r, "send")
    a2a_wait(ws_gu, wr_gu, wgu_s, wgu_r, "send")
    a2a_wait(gs_dn, gr_dn, gdn_s, gdn_r, "send")
    a2a_wait(gs_gu, gr_gu, ggu_s, ggu_r, "send")
    for k in range(1, nz):
        zg(k).wait_send()
        rcopy(usum.at[z], z_in.at[k], zo_s.at[k], zo_r.at[k], d, other).wait_send()
    for k in range(1, ny):
        rcopy(
            xall.at[c, row_of(y)], xall.at[c, row_of(y)], yg_s.at[k], yg_r.at[k], d, other
        ).wait_send()
        rcopy(tsum.at[row_of(y)], y_in.at[k], yo_s.at[k], yo_r.at[k], d, other).wait_send()
    for k in range(ny):
        to_core(k).wait_send()
    for k in range(1, nx):
        dp_out(2 * fown, fown, k, ph_s, ph_r).wait_send()
        dp_out(0, 2 * fown, k, pg_s, pg_r).wait_send()
        rcopy(hid.at[:, my_tok], hid.at[:, my_tok], h_s.at[k], h_r.at[k], d, other).wait_send()
        rcopy(zs.at[0], zr.at[0], zx_s.at[k], zx_r.at[k], d, other).wait_send()
    core_out.wait_send()
    for q in range(nx):

        @pl.when(jnp.logical_not(is_self(q)))
        def _():
            rcopy(
                vsum.at[:, pl.ds(q * tk, tk)],
                f_in.at[c, d % dpc],
                fo_s.at[q],
                fo_r.at[c, d % dpc],
                q,
                fcore,
            ).wait_send()


def per_device(dims, tokens_in, out_grad, gate_blocks, up_blocks, down_blocks, gate_up_index, down_index):
    nx, ny, nz = dims
    nt, ne = gate_up_index.shape[:2]
    npl = ny * nz
    db = npl
    bs = gate_blocks.shape[1]
    tk = tokens_in.shape[0]
    own = dims_own(dims)
    rr = bs // nx
    dpc = nx // 2
    fown = own * bs
    tok = nx * tk
    cells = own * db
    me = lax.axis_index("tensor")
    tables = route_tables(
        (
            (gate_up_index[:, :, 1], gate_up_index[:, :, 0]),
            (down_index[:, :, 0], down_index[:, :, 1]),
        ),
        own,
        db,
        me,
    )
    v = lambda *s: pltpu.VMEM(s, BF)
    dma = lambda *s: pltpu.SemaphoreType.DMA(s)
    scratch = [
        v(2, ne + 1, rr, bs),
        v(ne, bs, bs),
        v(ne + 1, rr, bs),
        v(2, dpc, rr, tk),
        v(nt, 2, rr, bs),
        v(nt + 1, 2, rr, bs),
        v(nt, rr, bs),
        v(nt + 1, rr, bs),
        v(2, npl, rr, tok),
        v(db, rr, 3 * fown),
        v(3 * fown, tok),
        v(nx, 3 * fown, tk),
        v(3 * fown, tok),
        v(2, npl, rr, tok),
        v(npl, rr, tok),
        v(npl, rr, tok),
        v(ny, nz, rr, tok),
        v(nz, rr, tok),
        v(nz, rr, tok),
        v(rr, tok),
        v(2, dpc, rr, tk),
        v(cells, 2, rr, bs),
        v(cells, rr, bs),
        v(nt, 2, rr, bs),
        v(nt, 2, rr, bs),
        v(nt, rr, bs),
        v(nt, rr, bs),
        v(ne // nx, rr, nx * bs),
        v(nx, ne // nx, rr, bs),
        v(nx, ne // nx, rr, bs),
        dma(3),
        dma(2, dpc),
        dma(nx),
        dma(nz),
        dma(nz),
        dma(ny),
        dma(ny),
        dma(ny),
        dma(ny),
        pltpu.SemaphoreType.DMA,
        pltpu.SemaphoreType.DMA,
        pltpu.SemaphoreType.DMA,
        pltpu.SemaphoreType.DMA,
        dma(nx),
        dma(nx),
        dma(nx),
        dma(nx),
        dma(nx),
        dma(nx),
        pltpu.SemaphoreType.DMA,
        pltpu.SemaphoreType.DMA,
        dma(ny),
        dma(ny),
        dma(nz),
        dma(nz),
        dma(nx),
        dma(2, dpc),
        pltpu.SemaphoreType.DMA,
        pltpu.SemaphoreType.DMA,
        pltpu.SemaphoreType.DMA,
        pltpu.SemaphoreType.DMA,
        dma(nx),
        dma(nx),
    ]
    vm = pl.BlockSpec(memory_space=pltpu.VMEM)
    hbm = pl.BlockSpec(memory_space=pl.ANY)
    grad = jax.ShapeDtypeStruct((ne, rr, bs), BF)
    act = jax.ShapeDtypeStruct(tokens_in.shape, BF)
    return pl.pallas_call(
        functools.partial(kernel, (nx, ny, nz, ne, own, db)),
        out_shape=(act, act, grad, grad, grad),
        in_specs=[pl.BlockSpec(memory_space=pltpu.SMEM), vm, vm, hbm, hbm, hbm],
        out_specs=(vm,) * 5,
        scratch_shapes=scratch,
        compiler_params=pltpu.CompilerParams(
            collective_id=0, has_side_effects=True, vmem_limit_bytes=56 * 2**20
        ),
    )(tables, tokens_in, out_grad, gate_blocks, up_blocks, down_blocks)


FB = 128
GRID = {4: (4, 8)}


def dims_own(dims):
    return FB // (dims[1] * dims[2] * 2)


def solution(mesh):
    nx, nt = mesh.shape["dp"], mesh.shape["tensor"]
    ny, nz = GRID[nx]
    in_specs = (
        P("dp", "tensor"),
        P("dp", "tensor"),
        P("tensor", None, None),
        P("tensor", None, None),
        P("tensor", None, None),
        P(),
        P(),
    )
    out_specs = (
        P("dp", "tensor"),
        P("dp", "tensor"),
        P("tensor", "dp", None),
        P("tensor", "dp", None),
        P("tensor", "dp", None),
    )
    return jax.shard_map(
        functools.partial(per_device, (nx, ny, nz)),
        mesh=mesh,
        in_specs=in_specs,
        out_specs=out_specs,
        check_vma=False,
    )
```

time: 845 us -> 145 us (0.17)
  waiting for transfers between devices: 699 us -> 0 us
  Pallas kernels: 0 us -> 134 us
  local copies, waits for them, and re-layouts: 60 us -> 9.45 us
  matrix products: 29.8 us -> 0 us
  starting transfers between devices: 20.2 us -> 0 us
  other arithmetic: 19.5 us -> 0.35 us
  between operations: 14.4 us -> 0.69 us
    reduce_scatter x5 -> x0, waiting for transfers between devices: 337 us -> none  [the longest x1 142 us: per_device(): lax.psum_scatter(out_dense.reshape(tok_rows, blocks_d * block_size), 'ten...]
    all_to_all x3 -> x0, waiting for transfers between devices: 200 us -> none  [the longest x1 107 us: per_device(): lax.all_to_all(back_send, 'tensor', split_axis=1, concat_axis=1, tiled=True)]
    all_gather x3 -> x0, waiting for transfers between devices: 161 us -> none  [the longest x1 80.5 us: per_device(): x_whole = lax.all_gather(tokens_in, 'tensor', axis=1, tiled=True)]
    pallas_call x0 -> x1, Pallas kernels: none -> 134 us  [per_device(): pl.pallas_call(functools.partial(kernel, (nx, ny, nz, ne, own, db)), out_...]
    dot_general x11 -> x0, matrix products: 29.8 us -> none  [the longest x1 4.53 us: per_device(): jnp.einsum('rsf,sl->rlf', arrived, gu_onehot, precision=lax.Precision.HIG...]
    all_to_all x3 -> x0, starting transfers between devices: 19.7 us -> none  [the longest x1 6.89 us: per_device(): lax.all_to_all(outgoing.astype(jnp.bfloat16), 'tensor', split_axis=1, con...]
    gather x5 -> x0, local copies, waits for them, and re-layouts: 14.6 us -> none  [the longest x1 4.26 us: per_device(): gu_sel = jnp.take(returned, gu_slot, axis=1)]
    scatter x2 -> x0, local copies, waits for them, and re-layouts: 13.7 us -> none  [the longest x1 8.33 us: per_device(): jnp.zeros((tok_rows, slot_total, 2 * block_size), jnp.float32)]
  transfers between devices with their start and end apart: 11 -> 0, of which waited for: 9 -> 0; matrix products, arithmetic and copies ran while one was open for 9% -> 0% of each run, Pallas kernels for 0% -> 0%
where the time goes in v1:
time: 145 us
  Pallas kernels  134 us (92%)
  local copies, waits for them, and re-layouts  9.45 us (7%)
    pallas_call x1, Pallas kernels, per_device(): pl.pallas_call(functools.partial(kernel, (nx, ny, nz, ne, own, db)), out_...  134 us
    unnamed x17, local copies, waits for them, and re-layouts  6.39 us

profile of v1, /device:TPU:1, one launch (start us, length us, event | category | flops | bytes accessed | tf_op | source)
XLA Modules:
  0.0 144.5 jit_solution(12559985918624185694)
XLA Ops:
  0.6 0.0 copy-start.5
  0.6 1.4 copy.29.x_ref
  2.1 0.0 copy-done.5
  2.1 0.0 copy-start.3
  2.1 0.7 copy.30.dy_ref
  2.8 0.0 copy-done.3
  2.8 0.0 copy-start.4
  2.9 0.7 copy-done.4
  3.6 0.1 fusion.3
  3.7 0.2 dynamic-slice_reduce_fusion
  3.9 0.1 select_reduce_fusion.1
  4.0 0.1 select_reduce_fusion
  4.1 0.1 pad_add_fusion.1
  4.2 0.7 reshape.14.idx
  4.9 134.0 %shard_map.110 = (bf16[128,64]{1,0:T(8,128)(2,1)}, bf16[128,64]{1,0:T(8,128)(2,1)}, bf16[32,32,128]{2,1,0:T(8,128)(2,1)}, bf16[32,32,128]{2,1,0:T(8,128)(2,1)}, bf16[32,32,128]{2,1,0:T(8,128)(2,1)}) custom-call(s32[448]{0:T(512)} %reshape.14.idx, bf16[128,64]{1,0:T(8,128)(2,1)} %copy.29.x_ref, bf16[128,64]{1,0:T(8,128)(2,1)} %copy.30.dy_ref, ...), custom_call_target="tpu_custom_call" | custom-call | tf_op jit(solution)/shard_map/pallas_call | solution.py:740
  138.9 0.0 copy-start.2
  138.9 1.5 %copy.31 = bf16[128,64]{0,1:T(8,128)(2,1)} copy(bf16[128,64]{1,0:T(8,128)(2,1)} %get-tuple-element.15) | data formatting | bytes 32768 | tf_op jit(solution)/shard_map/pallas_call | solution.py:740
  140.3 0.0 copy-done.2
  140.3 0.7 copy.32
  141.0 0.0 copy-start.1
  141.0 1.7 %copy.39 = bf16[32,32,128]{2,1,0:T(8,128)(2,1)} copy(bf16[32,32,128]{2,1,0:T(8,128)(2,1)} %get-tuple-element.33) | data formatting | bytes 524288
  142.8 0.0 copy-done.1
  142.8 0.0 copy-start
  142.8 0.7 copy.40
  143.5 0.3 copy-done
  143.8 0.7 copy.41
  (3 shorter events, 0.1 us)
Async XLA Ops:
  0.6 1.5 %copy-start.5 = (bf16[128,64]{0,1:T(8,128)(2,1)S(1)}, bf16[128,64]{0,1:T(8,128)(2,1)}, u32[]{:S(2)}) copy-start(bf16[128,64]{0,1:T(8,128)(2,1)} %param.8) | copy-start | bytes 49156
  2.1 0.8 copy-start.3
  2.8 0.8 copy-start.4
  138.9 1.5 %copy-start.2 = (bf16[128,64]{1,0:T(8,128)(2,1)S(1)}, bf16[128,64]{1,0:T(8,128)(2,1)}, u32[]{:S(2)}) copy-start(bf16[128,64]{1,0:T(8,128)(2,1)} %get-tuple-element.16) | copy-start | bytes 49156
  141.0 1.7 %copy-start.1 = (bf16[32,32,128]{2,1,0:T(8,128)(2,1)S(1)}, bf16[32,32,128]{2,1,0:T(8,128)(2,1)}, u32[]{:S(2)}) copy-start(bf16[32,32,128]{2,1,0:T(8,128)(2,1)} %get-tuple-element.34) | copy-start | bytes 786436
  142.8 1.0 copy-start

commit v2 on v1

v2 whole, which is shorter than its diff:
```python
import functools

import jax
import jax.numpy as jnp
from jax import lax
from jax.experimental import pallas as pl
from jax.experimental.pallas import tpu as pltpu
from jax.sharding import PartitionSpec as P

MESH = pl.DeviceIdType.MESH
BF = jnp.bfloat16
F32 = jnp.float32


def route_tables(lists, own, width_blocks, me):
    key = jnp.stack([k for k, _ in lists])
    other = jnp.stack([o for _, o in lists])
    nt, ne = key.shape[1:]
    owner = key // own
    cell = (key % own) * width_blocks + other
    my_owner = lax.dynamic_index_in_dim(owner, me, 1, keepdims=False)
    hit = my_owner[:, None, :] == jnp.arange(nt)[None, :, None]
    send = jnp.min(jnp.where(hit, jnp.arange(ne)[None, None, :], ne), axis=2)
    ret = jnp.max(jnp.where(owner == me, cell, -1), axis=2)
    match = ret[:, None, :] == jnp.arange(own * width_blocks)[None, :, None]
    source = jnp.min(jnp.where(match, jnp.arange(nt)[None, None, :], nt), axis=2)
    table = jnp.concatenate([send, source, jnp.maximum(ret, 0), my_owner], axis=1)
    return table.astype(jnp.int32).reshape(-1)


def kernel(
    cfg,
    idx,
    x_hbm,
    dy_hbm,
    gate_hbm,
    up_hbm,
    down_hbm,
    out_ref,
    in_ref,
    gg_ref,
    ug_ref,
    dg_ref,
    gu_in,
    gu_ab,
    dn_in,
    dn_t,
    xs,
    ws_gu,
    wr_a,
    wr_b,
    ws_dn,
    wr_dn,
    xall,
    wd,
    part,
    psum_in,
    part_d,
    psum_d,
    hid_g,
    hid_d,
    oall,
    c_in,
    tsum,
    y_in,
    usum,
    z_in,
    vsum,
    f_in,
    gc,
    gd,
    gs_gu,
    gr_gu,
    gs_dn,
    gr_dn,
    stage,
    zl,
    zs,
    zr,
    load_sem,
    dpx_s,
    dpx_r,
    zg_s,
    zg_r,
    yg_s,
    yg_r,
    cg_s,
    cg_r,
    wdn_s,
    wdn_r,
    wgu_s,
    wgu_r,
    ph_s,
    ph_r,
    pd_s,
    pd_r,
    hg_s,
    hg_r,
    hd_s,
    hd_r,
    co_s,
    co_r,
    yo_s,
    yo_r,
    zo_s,
    zo_r,
    fo_s,
    fo_r,
    gdn_s,
    gdn_r,
    ggu_s,
    ggu_r,
    zx_s,
    zx_r,
):
    nx, ny, nz, ne, own, db = cfg
    wr_gu = (wr_a, wr_b)
    nt = ny * nz * 2
    npl = ny * nz
    bs = 128
    hb = bs // 2
    tk = 128
    rr = bs // nx
    dpc = nx // 2
    fown = own * bs
    cells = own * db
    stride = nt + cells + nt + ne
    tok = nx * tk
    kall = db * rr
    d = lax.axis_index("dp")
    t = lax.axis_index("tensor")
    c = t % 2
    chip = t // 2
    y = chip // nz
    z = chip % nz
    other = chip * 2 + 1 - c
    my_tok = pl.ds(pl.multiple_of(d * tk, tk), tk)
    nt_dims = (((1,), (1,)), ((), ()))
    tn_dims = (((0,), (0,)), ((), ()))

    def onehot(shape, fn):
        return fn(
            lax.broadcasted_iota(jnp.int32, shape, 0), lax.broadcasted_iota(jnp.int32, shape, 1)
        ).astype(F32).astype(BF)

    def rcopy(src, dst, ssem, rsem, dd, tt):
        return pltpu.make_async_remote_copy(
            src_ref=src,
            dst_ref=dst,
            send_sem=ssem,
            recv_sem=rsem,
            device_id=(dd, tt),
            device_id_type=MESH,
        )

    barrier = pltpu.get_barrier_semaphore()

    rows = pl.ds(pl.multiple_of(d * rr, rr), rr)
    loads = [
        pltpu.make_async_copy(gate_hbm.at[:, rows, :], gu_in.at[0], load_sem.at[0]),
        pltpu.make_async_copy(up_hbm.at[:, rows, :], gu_in.at[1], load_sem.at[1]),
        pltpu.make_async_copy(x_hbm, xs.at[0], load_sem.at[2]),
        pltpu.make_async_copy(dy_hbm, xs.at[1], load_sem.at[3]),
        pltpu.make_async_copy(down_hbm, dn_in, load_sem.at[4]),
    ]
    for cp in loads:
        cp.start()

    @pl.loop(1, nt)
    def _(i):
        pl.semaphore_signal(
            barrier, inc=1, device_id=(d, lax.rem(t + i, nt)), device_id_type=MESH
        )

    for k in range(1, nx):
        for cc in range(2):
            pl.semaphore_signal(
                barrier,
                inc=1,
                device_id=(lax.rem(d + k, nx), chip * 2 + cc),
                device_id_type=MESH,
            )

    zero_rows = jnp.zeros((rr, bs), BF)
    dn_t[ne] = zero_rows
    wr_dn[nt] = zero_rows
    for h in range(2):
        gu_ab[h, ne] = zero_rows
        wr_gu[h][nt] = zero_rows

    def half_src(i):
        return (i % bs) // hb * bs + i // bs * hb + i % hb

    halves = onehot((2 * bs, 2 * bs), lambda r, q: r == half_src(q))
    loads[0].wait()
    loads[1].wait()
    me_n = 256 // rr

    @pl.loop(0, ne // me_n)
    def _(i):
        es = pl.ds(i * me_n, me_n)
        both = jnp.concatenate(
            [gu_in[0, es].reshape(me_n * rr, bs), gu_in[1, es].reshape(me_n * rr, bs)], axis=1
        )
        res = jnp.dot(both, halves, preferred_element_type=F32).astype(BF)
        for h in range(2):
            gu_ab[h, es] = res[:, h * bs : (h + 1) * bs].reshape(me_n, rr, bs)

    @pl.loop(0, nt)
    def _(s):
        e = idx[s]
        ws_gu[0, s] = gu_ab[0, e]
        ws_gu[1, s] = gu_ab[1, e]

    for h in range(2):
        wr_gu[h][t] = ws_gu[h, t]

    loads[2].wait()
    loads[3].wait()
    pl.semaphore_wait(barrier, nt - 1 + 2 * (nx - 1))

    def dpx(a, j, go):
        dst_d = c * dpc + j
        is_me = jnp.logical_and(dst_d == d, c == a)

        @pl.when(jnp.logical_not(is_me))
        def _():
            go(
                rcopy(
                    xs.at[a, j],
                    xall.at[a, chip, :, my_tok],
                    dpx_s.at[a, j],
                    dpx_r.at[d],
                    dst_d,
                    chip * 2 + a,
                )
            )

    for a in range(2):
        for j in range(dpc):
            dpx(a, j, lambda cp: cp.start())

    @pl.when(d // dpc == c)
    def _():
        xall[c, chip, :, my_tok] = xs[c, d % dpc]

    def a2a(src, dst, ssem, rsem, lo, hi):
        @pl.loop(lo, hi)
        def _(i):
            to = lax.rem(t + i, nt)
            rcopy(src.at[to], dst.at[t], ssem, rsem, d, to).start()

    def a2a_all(src, dst, ssem, rsem):
        return rcopy(
            src.at[pl.ds(0, nt - 1)], dst.at[pl.ds(0, nt - 1)], ssem, rsem, d, lax.rem(t + 1, nt)
        )

    def gu_out(h):
        return ws_gu.at[h], wr_gu[h], wgu_s.at[h], wgu_r.at[h]

    dn_out = (ws_dn, wr_dn, wdn_s, wdn_r)
    mid = nt // 2

    loads[4].wait()
    pick = onehot((rr, bs), lambda r, q: q == r + d * rr)
    en = 8 if ne % 8 == 0 else ne

    @pl.loop(0, ne // en)
    def _(i):
        blocks = dn_in[pl.ds(i * en, en)].reshape(en * bs, bs)
        res = lax.dot_general(pick, blocks, nt_dims, preferred_element_type=F32).astype(BF)
        for k in range(en):
            dn_t[i * en + k] = res[:, k * bs : (k + 1) * bs]

    @pl.loop(0, nt)
    def _(s):
        ws_dn[s] = dn_t[idx[stride + s]]

    wr_dn[t] = ws_dn[t]

    for q in range(nx):

        @pl.when(jnp.logical_not(jnp.logical_and(q == d, d // dpc == c)))
        def _():
            rcopy(
                xs.at[0, 0],
                xall.at[c, chip, :, pl.ds(q * tk, tk)],
                dpx_s.at[0, 0],
                dpx_r.at[q],
                d,
                other,
            ).wait_recv()

    def zg(k):
        return rcopy(
            xall.at[c, chip],
            xall.at[c, chip],
            zg_s.at[k],
            zg_r.at[k],
            d,
            (y * nz + lax.rem(z + k, nz)) * 2 + c,
        )

    for k in range(1, nz):
        zg(k).start()
    a2a(*gu_out(0), 1, nt)


    for k in range(1, nz):
        rcopy(
            xall.at[c, chip],
            xall.at[c, y * nz + lax.rem(z - k + nz, nz)],
            zg_s.at[k],
            zg_r.at[k],
            d,
            other,
        ).wait_recv()

    def row_of(yy):
        return pl.ds(yy * nz, nz)

    def yg(k):
        yy = lax.rem(y + k, ny)
        return rcopy(
            xall.at[c, row_of(y)],
            xall.at[c, row_of(y)],
            yg_s.at[k],
            yg_r.at[k],
            d,
            (yy * nz + z) * 2 + c,
        )

    def to_core(k, arr):
        yy = lax.rem(y - k + ny, ny)
        return rcopy(
            xall.at[c, row_of(yy)], xall.at[arr, row_of(yy)], cg_s.at[k], cg_r.at[k], d, other
        )

    for k in range(1, ny):
        yg(k).start()
    to_core(0, c).start()
    a2a(*dn_out, 1, nt)

    for k in range(1, ny):
        yy = lax.rem(y - k + ny, ny)
        rcopy(
            xall.at[c, row_of(y)],
            xall.at[c, row_of(yy)],
            yg_s.at[k],
            yg_r.at[k],
            d,
            other,
        ).wait_recv()
        to_core(k, c).start()
    a2a(*gu_out(1), 1, nt)
    for k in range(ny):
        to_core(k, 1 - c).wait_recv()

    def partials(lo, arr, store):
        @pl.loop(0, own)
        def _(f):
            cols = pl.ds(pl.multiple_of(lo + f * bs, bs), bs)
            lhs = wd[:, :, cols].reshape(kall, bs)
            rhs = xall[arr].reshape(kall, tok)
            store(f, lax.dot_general(lhs, rhs, tn_dims, preferred_element_type=F32).astype(BF))

    def partials_gu(h):
        def store(f, res):
            part[h, pl.ds(pl.multiple_of(f * bs, bs), bs), :] = res

        partials((1 + h) * fown, 0, store)

    def store_hg(f, res):
        part_d[f] = res.reshape(2, hb, tok)

    def dp_out(h, k):
        dd = lax.rem(d + k, nx)
        dst_tok = pl.ds(pl.multiple_of(dd * tk, tk), tk)
        return (
            rcopy(
                part.at[h, :, dst_tok], psum_in.at[k, h], ph_s.at[h, k], ph_r.at[h, k], dd, t
            ),
            rcopy(
                part_d.at[:, h, :, dst_tok],
                psum_d.at[k, :, h],
                pd_s.at[h, k],
                pd_r.at[h, k],
                dd,
                t,
            ),
        )

    def dp_send(h):
        for k in range(1, nx):
            for cp in dp_out(h, k):
                cp.start()

    def dp_wait(h):
        for k in range(1, nx):
            for cp in dp_out(h, k):
                cp.wait_recv()

    def unpack_gu(h):
        @pl.loop(0, db)
        def _(a):
            for jl in range(own):
                s = idx[nt + jl * db + a]
                wd[a, :, pl.ds((1 + h) * fown + jl * bs, bs)] = wr_gu[h][s]

    a2a_all(*gu_out(0)).wait_recv()
    unpack_gu(0)
    partials_gu(0)

    a2a_all(*dn_out).wait_recv()

    @pl.loop(0, db)
    def _(a):
        for jl in range(own):
            s = idx[stride + nt + jl * db + a]
            wd[a, :, pl.ds(jl * bs, bs)] = wr_dn[s]

    partials(0, 1, store_hg)
    dp_send(0)

    def activations(h):
        @pl.loop(0, own)
        def _(j):
            def total(read, peer):
                acc = read().astype(F32)
                for k in range(1, nx):
                    acc += peer(k).astype(F32)
                return acc

            def gu_total(lo):
                r = pl.ds(pl.multiple_of(j * bs + lo, hb), hb)
                return total(lambda: part[h, r, my_tok], lambda k: psum_in[k, h, r, :])

            gate = gu_total(0)
            up = gu_total(hb)
            hg = total(lambda: part_d[j, h, :, my_tok], lambda k: psum_d[k, j, h])
            sig = 1.0 / (1.0 + jnp.exp(-gate))
            act = gate * sig
            hid_d[j, h, :, my_tok] = (act * up).astype(BF)
            g0 = pl.multiple_of(j * bs, bs)
            hid_g[h, pl.ds(g0, hb), my_tok] = (
                hg * up * sig * (1.0 + gate * (1.0 - sig))
            ).astype(BF)
            hid_g[h, pl.ds(g0 + hb, hb), my_tok] = (hg * act).astype(BF)

    def h_copies(h, k, src):
        tok_src = pl.ds(pl.multiple_of(src * tk, tk), tk)
        dd = lax.rem(d + k, nx)
        return (
            rcopy(
                hid_g.at[h, :, my_tok], hid_g.at[h, :, tok_src], hg_s.at[h, k], hg_r.at[h, k], dd, t
            ),
            rcopy(
                hid_d.at[:, h, :, my_tok],
                hid_d.at[:, h, :, tok_src],
                hd_s.at[h, k],
                hd_r.at[h, k],
                dd,
                t,
            ),
        )

    def h_send(h):
        for k in range(1, nx):
            for cp in h_copies(h, k, d):
                cp.start()

    def h_wait(h):
        for k in range(1, nx):
            for cp in h_copies(h, k, lax.rem(d - k + nx, nx)):
                cp.wait_recv()

    dp_wait(0)
    activations(0)
    h_send(0)

    a2a_all(*gu_out(1)).wait_recv()
    unpack_gu(1)
    partials_gu(1)
    dp_send(1)

    mt = 256 // rr

    def grads(arr, rhs, store):
        @pl.loop(0, db // mt)
        def _(i):
            lhs = xall[arr, pl.ds(i * mt, mt)].reshape(mt * rr, tok)
            res = lax.dot_general(lhs, rhs(), nt_dims, preferred_element_type=F32).astype(BF)
            for jl in range(own):
                store(jl * db + i * mt, res[:, jl * bs : (jl + 1) * bs].reshape(mt, rr, bs))

    def grads_gu(h):
        def store(c0, v):
            gc[h, pl.ds(c0, mt)] = v

        grads(0, lambda: hid_g[h], store)

        @pl.loop(0, nt)
        def _(s):
            gs_gu[h, s] = gc[h, idx[nt + cells + s]]

        gr_gu[h, t] = gs_gu[h, t]

    def gu_back(h):
        return gs_gu.at[h], gr_gu.at[h], ggu_s.at[h], ggu_r.at[h]

    dn_back = (gs_dn, gr_dn, gdn_s, gdn_r)

    h_wait(0)
    grads_gu(0)
    a2a(*gu_back(0), 1, nt)

    dp_wait(1)
    activations(1)
    h_send(1)

    h_wait(1)

    @pl.loop(0, db // mt)
    def _(i):
        arows = pl.ds(i * mt, mt)
        lhs = wd[arows, :, pl.ds(0, fown)].reshape(mt * rr, fown)
        res = jnp.dot(lhs, hid_d[...].reshape(fown, tok), preferred_element_type=F32)
        oall[0, arows] = res.astype(BF).reshape(mt, rr, tok)
        lhs = wd[arows, :, pl.ds(fown, 2 * fown)].reshape(mt * rr, 2 * fown)
        res = jnp.dot(lhs, hid_g[...].reshape(2 * fown, tok), preferred_element_type=F32)
        oall[1, arows] = res.astype(BF).reshape(mt, rr, tok)

    core_out = rcopy(oall.at[1 - c], c_in, co_s, co_r, d, other)
    core_out.start()

    def store_dn(c0, v):
        gd[pl.ds(c0, mt)] = v

    grads(1, lambda: hid_d[...].reshape(fown, tok), store_dn)

    @pl.loop(0, nt)
    def _(s):
        gs_dn[s] = gd[idx[stride + nt + cells + s]]

    gr_dn[t] = gs_dn[t]
    a2a(*dn_back, 1, nt)

    core_out.wait_recv()

    @pl.loop(0, npl)
    def _(p):
        tsum[p] = (oall[c, p].astype(F32) + c_in[p].astype(F32)).astype(BF)

    def yo(k):
        yy = lax.rem(y + k, ny)
        return rcopy(
            tsum.at[row_of(yy)], y_in.at[k], yo_s.at[k], yo_r.at[k], d, (yy * nz + z) * 2 + c
        )

    for k in range(1, ny):
        yo(k).start()

    grads_gu(1)
    a2a(*gu_back(1), 1, mid)

    for k in range(1, ny):
        yo(k).wait_recv()

    @pl.loop(0, nz)
    def _(p):
        acc = tsum[y * nz + p].astype(F32)
        for k in range(1, ny):
            acc += y_in[k, p].astype(F32)
        usum[p] = acc.astype(BF)

    def zo(k):
        zz = lax.rem(z + k, nz)
        return rcopy(
            usum.at[zz], z_in.at[k], zo_s.at[k], zo_r.at[k], d, (y * nz + zz) * 2 + c
        )

    for k in range(1, nz):
        zo(k).start()
    a2a(*gu_back(1), mid, nt)

    a2a_all(*dn_back).wait_recv()
    groups = ne // nx

    @pl.loop(0, groups)
    def _(g):
        for p in range(nx):
            o = idx[stride + nt + cells + nt + g * nx + p]
            zl[g, :, pl.ds(p * bs, bs)] = gr_dn[o]

    for dd in range(nx):
        perm = onehot(
            (nx * bs, bs), lambda r, q: r == (q // rr) * bs + dd * rr + q % rr
        )
        moved = jnp.dot(zl[...].reshape(groups * rr, nx * bs), perm, preferred_element_type=F32)
        zs[dd] = moved.astype(BF).reshape(groups, rr, bs)
    zr[d] = zs[d]

    def zx(k, src):
        dd = lax.rem(d + k, nx)
        return rcopy(zs.at[dd], zr.at[src], zx_s.at[k], zx_r.at[k], dd, t)

    for k in range(1, nx):
        zx(k, d).start()

    for k in range(1, nz):
        zo(k).wait_recv()
    acc = usum[z].astype(F32)
    for k in range(1, nz):
        acc += z_in[k].astype(F32)
    vsum[...] = acc.astype(BF)

    def fo(q):
        return rcopy(
            vsum.at[:, pl.ds(q * tk, tk)],
            f_in.at[c, d % dpc],
            fo_s.at[q],
            fo_r.at[c, d % dpc],
            q,
            chip * 2 + d // dpc,
        )

    def unless_self(q, go):
        @pl.when(jnp.logical_not(jnp.logical_and(q == d, d // dpc == c)))
        def _():
            go(fo(q))

    for q in range(nx):
        unless_self(q, lambda cp: cp.start())

    @pl.when(d // dpc == c)
    def _():
        f_in[c, d % dpc] = vsum[:, my_tok]

    for k in range(1, nx):
        zx(k, lax.rem(d - k + nx, nx)).wait_recv()
    eye_b = onehot((bs, bs), lambda r, q: r == q)

    @pl.loop(0, groups)
    def _(g):
        block = zr[:, g].reshape(nx * rr, bs)
        flip = lax.dot_general(block, eye_b, tn_dims, preferred_element_type=F32)
        dg_ref[pl.ds(g * nx, nx)] = flip.astype(BF).reshape(nx, rr, bs)

    for a in range(2):
        for j in range(dpc):
            src_d = c * dpc + j
            own_piece = jnp.logical_and(src_d == d, a == c)

            @pl.when(jnp.logical_not(own_piece))
            def _():
                rcopy(
                    vsum.at[:, pl.ds(0, tk)],
                    f_in.at[a, j],
                    fo_s.at[0],
                    fo_r.at[a, j],
                    d,
                    other,
                ).wait_recv()

    for a, ref in enumerate((out_ref, in_ref)):
        ref[...] = f_in[a]

    for h in range(2):
        a2a_all(*gu_back(h)).wait_recv()

    @pl.loop(0, ne)
    def _(e):
        o = idx[nt + cells + nt + e]
        for h in range(2):
            stage[e, :, pl.ds(h * bs, bs)] = gr_gu[h, o]

    @pl.loop(0, ne // me_n)
    def _(i):
        es = pl.ds(i * me_n, me_n)
        both = stage[es].reshape(me_n * rr, 2 * bs)
        res = jnp.dot(both, halves, preferred_element_type=F32).astype(BF)
        gg_ref[es] = res[:, :bs].reshape(me_n, rr, bs)
        ug_ref[es] = res[:, bs:].reshape(me_n, rr, bs)

    for a in range(2):
        for j in range(dpc):
            dpx(a, j, lambda cp: cp.wait_send())
    for h in range(2):
        a2a_all(*gu_out(h)).wait_send()
        a2a_all(*gu_back(h)).wait_send()
    a2a_all(*dn_out).wait_send()
    a2a_all(*dn_back).wait_send()
    for k in range(1, nz):
        zg(k).wait_send()
        zo(k).wait_send()
    for k in range(1, ny):
        yg(k).wait_send()
        yo(k).wait_send()
    for k in range(ny):
        to_core(k, c).wait_send()
    for k in range(1, nx):
        for h in range(2):
            for cp in dp_out(h, k) + h_copies(h, k, d):
                cp.wait_send()
        zx(k, d).wait_send()
    core_out.wait_send()
    for q in range(nx):
        unless_self(q, lambda cp: cp.wait_send())


def copy_kernel(n, *refs):
    for i in range(n):
        refs[n + i][...] = refs[i][...]


def per_device(dims, tokens_in, out_grad, gate_blocks, up_blocks, down_blocks, gate_up_index, down_index):
    nx, ny, nz = dims
    nt, ne = gate_up_index.shape[:2]
    npl = ny * nz
    db = npl
    bs = gate_blocks.shape[1]
    tk = tokens_in.shape[0]
    own = FB // nt
    rr = bs // nx
    dpc = nx // 2
    fown = own * bs
    tok = nx * tk
    cells = own * db
    tables = route_tables(
        (
            (gate_up_index[:, :, 1], gate_up_index[:, :, 0]),
            (down_index[:, :, 0], down_index[:, :, 1]),
        ),
        own,
        db,
        lax.axis_index("tensor"),
    )
    v = lambda *s: pltpu.VMEM(s, BF)
    dma = lambda *s: pltpu.SemaphoreType.DMA(s)
    scratch = [
        v(2, ne, rr, bs),
        v(2, ne + 1, rr, bs),
        v(ne, bs, bs),
        v(ne + 1, rr, bs),
        v(2, dpc, rr, tk),
        v(2, nt, rr, bs),
        v(nt + 1, rr, bs),
        v(nt + 1, rr, bs),
        v(nt, rr, bs),
        v(nt + 1, rr, bs),
        v(2, npl, rr, tok),
        v(db, rr, 3 * fown),
        v(2, fown, tok),
        v(nx, 2, fown, tk),
        v(own, 2, bs // 2, tok),
        v(nx, own, 2, bs // 2, tk),
        v(2, fown, tok),
        v(own, 2, bs // 2, tok),
        v(2, npl, rr, tok),
        v(npl, rr, tok),
        v(npl, rr, tok),
        v(ny, nz, rr, tok),
        v(nz, rr, tok),
        v(nz, rr, tok),
        v(rr, tok),
        v(2, dpc, rr, tk),
        v(2, cells, rr, bs),
        v(cells, rr, bs),
        v(2, nt, rr, bs),
        v(2, nt, rr, bs),
        v(nt, rr, bs),
        v(nt, rr, bs),
        v(ne, rr, 2 * bs),
        v(ne // nx, rr, nx * bs),
        v(nx, ne // nx, rr, bs),
        v(nx, ne // nx, rr, bs),
        dma(5),
        dma(2, dpc),
        dma(nx),
        dma(nz),
        dma(nz),
        dma(ny),
        dma(ny),
        dma(ny),
        dma(ny),
        pltpu.SemaphoreType.DMA,
        pltpu.SemaphoreType.DMA,
        dma(2),
        dma(2),
        dma(2, nx),
        dma(2, nx),
        dma(2, nx),
        dma(2, nx),
        dma(2, nx),
        dma(2, nx),
        dma(2, nx),
        dma(2, nx),
        pltpu.SemaphoreType.DMA,
        pltpu.SemaphoreType.DMA,
        dma(ny),
        dma(ny),
        dma(nz),
        dma(nz),
        dma(nx),
        dma(2, dpc),
        pltpu.SemaphoreType.DMA,
        pltpu.SemaphoreType.DMA,
        dma(2),
        dma(2),
        dma(nx),
        dma(nx),
    ]
    vm = pl.BlockSpec(memory_space=pltpu.VMEM)
    hbm = pl.BlockSpec(memory_space=pl.ANY)
    grad = jax.ShapeDtypeStruct((ne, rr, bs), BF)
    act = jax.ShapeDtypeStruct((dpc, rr, tk), BF)
    feat = dpc * rr
    shapes = (act, act, grad, grad, grad)
    results = pl.pallas_call(
        functools.partial(kernel, (nx, ny, nz, ne, own, db)),
        out_shape=shapes,
        in_specs=[pl.BlockSpec(memory_space=pltpu.SMEM)] + [hbm] * 5,
        out_specs=(vm,) * 5,
        scratch_shapes=scratch,
        compiler_params=pltpu.CompilerParams(
            collective_id=0, has_side_effects=True, vmem_limit_bytes=56 * 2**20
        ),
    )(
        tables,
        tokens_in.T.reshape(dpc, rr, tk),
        out_grad.T.reshape(dpc, rr, tk),
        gate_blocks,
        up_blocks,
        down_blocks,
    )
    n = len(shapes)
    results = pl.pallas_call(
        functools.partial(copy_kernel, n),
        out_shape=shapes,
        in_specs=[vm] * n,
        out_specs=(vm,) * n,
    )(*results)
    return tuple(r.reshape(feat, tk).T for r in results[:2]) + tuple(results[2:])


FB = 128
GRID = {4: (4, 8)}


def solution(mesh):
    nx, nt = mesh.shape["dp"], mesh.shape["tensor"]
    ny, nz = GRID[nx]
    in_specs = (
        P("dp", "tensor"),
        P("dp", "tensor"),
        P("tensor", None, None),
        P("tensor", None, None),
        P("tensor", None, None),
        P(),
        P(),
    )
    out_specs = (
        P("dp", "tensor"),
        P("dp", "tensor"),
        P("tensor", "dp", None),
        P("tensor", "dp", None),
        P("tensor", "dp", None),
    )
    return jax.shard_map(
        functools.partial(per_device, (nx, ny, nz)),
        mesh=mesh,
        in_specs=in_specs,
        out_specs=out_specs,
        check_vma=False,
    )
```

time: 145 us -> 127 us (0.88)
  Pallas kernels: 134 us -> 124 us
  local copies, waits for them, and re-layouts: 9.45 us -> 1.75 us
    pallas_call x1, Pallas kernels: 134 us -> 122 us  [per_device(): pl.pallas_call(functools.partial(kernel, (nx, ny, nz, ne, own, db)), out_...]
    unnamed x17 -> x2, local copies, waits for them, and re-layouts: 6.39 us -> 0.01 us
    pallas_call x2 -> x0, local copies, waits for them, and re-layouts: 2.15 us -> none  [per_device(): pl.pallas_call(functools.partial(kernel, (nx, ny, nz, ne, own, db)), out_...]
    pallas_call x0 -> x1, Pallas kernels: none -> 2.05 us  [per_device(): pl.pallas_call(functools.partial(copy_kernel, n), out_shape=shapes, in_sp...]
where the time goes in v2:
time: 127 us
  Pallas kernels  124 us (98%)
  local copies, waits for them, and re-layouts  1.75 us (1%)
    pallas_call x1, Pallas kernels, per_device(): pl.pallas_call(functools.partial(kernel, (nx, ny, nz, ne, own, db)), out_...  122 us

profile of v2, /device:TPU:1, one launch (start us, length us, event | category | flops | bytes accessed | tf_op | source)
XLA Modules:
  0.0 126.6 jit_solution(3873352345713487411)
XLA Ops:
  0.6 0.0 copy-start
  0.6 0.9 fusion.5
  1.5 0.0 copy-done
  1.6 0.1 fusion.3
  1.6 0.2 dynamic-slice_reduce_fusion
  1.8 0.1 select_reduce_fusion.1
  1.9 0.1 select_reduce_fusion
  2.0 0.1 pad_add_fusion.1
  2.1 0.7 reshape.26.idx
  2.8 121.8 %shard_map.110 = (bf16[2,32,128]{2,1,0:T(8,128)(2,1)}, bf16[2,32,128]{2,1,0:T(8,128)(2,1)}, bf16[32,32,128]{2,1,0:T(8,128)(2,1)}, bf16[32,32,128]{2,1,0:T(8,128)(2,1)}, bf16[32,32,128]{2,1,0:T(8,128)(2,1)}) custom-call(s32[448]{0:T(512)} %reshape.26.idx, bf16[2,32,128]{2,1,0:T(8,128)(2,1)} %bitcast.26, bf16[2,32,128]{2,1,0:T(8,128)(2,1)} %bitcast.27, ...), custom_call_target="tpu_custom_call" | custom-call | tf_op jit(solution)/shard_map/pallas_call | solution.py:819
  124.6 2.0 %shard_map.111 = (bf16[2,32,128]{2,1,0:T(8,128)(2,1)}, bf16[2,32,128]{2,1,0:T(8,128)(2,1)}, bf16[32,32,128]{2,1,0:T(8,128)(2,1)}, bf16[32,32,128]{2,1,0:T(8,128)(2,1)}, bf16[32,32,128]{2,1,0:T(8,128)(2,1)}) custom-call(bf16[2,32,128]{2,1,0:T(8,128)(2,1)} %get-tuple-element.15.refs_0_, bf16[2,32,128]{2,1,0:T(8,128)(2,1)} %get-tuple-element.16.refs_1_, ...), custom_call_target="tpu_custom_call" | custom-call | tf_op jit(solution)/shard_map/pallas_call | solution.py:837
  (2 shorter events, 0.0 us)
Async XLA Ops:
  0.6 0.9 copy-start

commit v3 on v2

v3 whole, which is shorter than its diff:
```python
import functools

import jax
import jax.numpy as jnp
from jax import lax
from jax.experimental import pallas as pl
from jax.experimental.pallas import tpu as pltpu
from jax.sharding import PartitionSpec as P

MESH = pl.DeviceIdType.MESH
BF = jnp.bfloat16
F32 = jnp.float32


def route_tables(lists, own, width_blocks, me):
    key = jnp.stack([k for k, _ in lists])
    other = jnp.stack([o for _, o in lists])
    nt, ne = key.shape[1:]
    owner = key // own
    cell = (key % own) * width_blocks + other
    my_owner = lax.dynamic_index_in_dim(owner, me, 1, keepdims=False)
    hit = my_owner[:, None, :] == jnp.arange(nt)[None, :, None]
    send = jnp.min(jnp.where(hit, jnp.arange(ne)[None, None, :], ne), axis=2)
    ret = jnp.max(jnp.where(owner == me, cell, -1), axis=2)
    match = ret[:, None, :] == jnp.arange(own * width_blocks)[None, :, None]
    source = jnp.min(jnp.where(match, jnp.arange(nt)[None, None, :], nt), axis=2)
    table = jnp.concatenate([send, source, jnp.maximum(ret, 0), my_owner], axis=1)
    return table.astype(jnp.int32).reshape(-1)


def kernel(
    cfg,
    idx,
    x_hbm,
    dy_hbm,
    gate_hbm,
    up_hbm,
    down_hbm,
    out_ref,
    in_ref,
    gg_ref,
    ug_ref,
    dg_ref,
    gu_in,
    gu_ab,
    dn_in,
    dn_t,
    xs,
    ws_gu,
    wr_a,
    wr_b,
    ws_dn,
    wr_dn,
    xall,
    wd,
    part,
    psum_in,
    part_d,
    psum_d,
    hid_g,
    hid_d,
    oall,
    c_in,
    tsum,
    y_in,
    usum,
    f_in,
    gc,
    gd,
    gs_gu,
    gr_a,
    gr_b,
    gs_dn,
    gr_dn,
    stage,
    zl,
    zs,
    zr,
    load_sem,
    xg_s,
    xg_r,
    yg_s,
    yg_r,
    cg_s,
    cg_r,
    wdn_s,
    wdn_r,
    wgu_s,
    wgu_r,
    ph_s,
    ph_r,
    pd_s,
    pd_r,
    hg_s,
    hg_r,
    hd_s,
    hd_r,
    co_s,
    co_r,
    yo_s,
    yo_r,
    fo_s,
    fo_r,
    gdn_s,
    gdn_r,
    ggu_s,
    ggu_r,
    zx_s,
    zx_r,
):
    nx, ny, nz, ne, own, db = cfg
    wr_gu = (wr_a, wr_b)
    gr_gu = (gr_a, gr_b)
    nt = ny * nz * 2
    npl = ny * nz
    bs = 128
    hb = bs // 2
    tk = 128
    rr = bs // nx
    dpc = nx // 2
    fown = own * bs
    cells = own * db
    stride = nt + cells + nt + ne
    tok = nx * tk
    kall = db * rr
    d = lax.axis_index("dp")
    t = lax.axis_index("tensor")
    c = t % 2
    chip = t // 2
    y = chip // nz
    z = chip % nz
    other = chip * 2 + 1 - c
    my_tok = pl.ds(pl.multiple_of(d * tk, tk), tk)
    nt_dims = (((1,), (1,)), ((), ()))
    tn_dims = (((0,), (0,)), ((), ()))

    def onehot(shape, fn):
        return fn(
            lax.broadcasted_iota(jnp.int32, shape, 0), lax.broadcasted_iota(jnp.int32, shape, 1)
        ).astype(F32).astype(BF)

    def rcopy(src, dst, ssem, rsem, dd, tt):
        return pltpu.make_async_remote_copy(
            src_ref=src,
            dst_ref=dst,
            send_sem=ssem,
            recv_sem=rsem,
            device_id=(dd, tt),
            device_id_type=MESH,
        )

    barrier = pltpu.get_barrier_semaphore()

    rows = pl.ds(pl.multiple_of(d * rr, rr), rr)
    loads = [
        pltpu.make_async_copy(gate_hbm.at[:, rows, :], gu_in.at[0], load_sem.at[0]),
        pltpu.make_async_copy(up_hbm.at[:, rows, :], gu_in.at[1], load_sem.at[1]),
        pltpu.make_async_copy(x_hbm, xs.at[0], load_sem.at[2]),
        pltpu.make_async_copy(dy_hbm, xs.at[1], load_sem.at[3]),
        pltpu.make_async_copy(down_hbm, dn_in, load_sem.at[4]),
    ]
    for cp in loads:
        cp.start()

    @pl.loop(1, nt)
    def _(i):
        pl.semaphore_signal(
            barrier, inc=1, device_id=(d, lax.rem(t + i, nt)), device_id_type=MESH
        )

    for k in range(1, nx):

        @pl.loop(0, 2 * nz)
        def _(i):
            pl.semaphore_signal(
                barrier,
                inc=1,
                device_id=(lax.rem(d + k, nx), y * nz * 2 + i),
                device_id_type=MESH,
            )

    loads[2].wait()
    loads[3].wait()
    pl.semaphore_wait(barrier, nt - 1 + 2 * nz * (nx - 1))

    my_half = pl.ds(pl.multiple_of(c * (tok // 2), tok // 2), tok // 2)
    its_half = pl.ds(pl.multiple_of((1 - c) * (tok // 2), tok // 2), tok // 2)

    def self_piece(plane, zz, core):
        return jnp.logical_and(jnp.logical_and(plane == d, zz == z), core == c)

    def x_out(a, j, zz, go):
        plane = c * dpc + j
        core = d // dpc

        @pl.when(jnp.logical_not(self_piece(plane, zz, core)))
        def _():
            go(
                rcopy(
                    xs.at[a, j],
                    xall.at[a, chip, :, my_tok],
                    xg_s.at[a, j, zz],
                    xg_r.at[a, z, d % dpc],
                    plane,
                    (y * nz + zz) * 2 + core,
                )
            )

    def x_out_all(a, go):
        for k in range(nz):
            for j in range(dpc):
                x_out(a, j, lax.rem(z + k, nz), go)

    def x_wait(a):
        for zz in range(nz):
            for j in range(dpc):
                q = c * dpc + j

                @pl.when(jnp.logical_not(self_piece(q, zz, d // dpc)))
                def _():
                    rcopy(
                        xs.at[0, 0],
                        xall.at[a, y * nz + zz, :, pl.ds(pl.multiple_of(q * tk, tk), tk)],
                        xg_s.at[0, 0, 0],
                        xg_r.at[a, zz, j],
                        d,
                        other,
                    ).wait_recv()

    x_out_all(0, lambda cp: cp.start())

    @pl.when(d // dpc == c)
    def _():
        for a in range(2):
            xall[a, chip, :, my_tok] = xs[a, d % dpc]

    zero_rows = jnp.zeros((rr, bs), BF)
    dn_t[ne] = zero_rows
    wr_dn[nt] = zero_rows
    for h in range(2):
        gu_ab[h, ne] = zero_rows
        wr_gu[h][nt] = zero_rows

    def half_src(i):
        return (i % bs) // hb * bs + i // bs * hb + i % hb

    halves = onehot((2 * bs, 2 * bs), lambda r, q: r == half_src(q))
    loads[0].wait()
    loads[1].wait()
    me_n = 256 // rr

    @pl.loop(0, ne // me_n)
    def _(i):
        es = pl.ds(i * me_n, me_n)
        both = jnp.concatenate(
            [gu_in[0, es].reshape(me_n * rr, bs), gu_in[1, es].reshape(me_n * rr, bs)], axis=1
        )
        res = jnp.dot(both, halves, preferred_element_type=F32).astype(BF)
        for h in range(2):
            gu_ab[h, es] = res[:, h * bs : (h + 1) * bs].reshape(me_n, rr, bs)

    @pl.loop(0, nt)
    def _(s):
        e = idx[s]
        ws_gu[0, s] = gu_ab[0, e]
        ws_gu[1, s] = gu_ab[1, e]

    for h in range(2):
        wr_gu[h][t] = ws_gu[h, t]

    row = 2 * nz

    def a2a_row(src, dst, ssem, rsem):
        @pl.loop(1, row)
        def _(i):
            to = y * row + lax.rem(t % row + i, row)
            rcopy(src.at[to], dst.at[t], ssem, rsem, d, to).start()

    def a2a_off(src, dst, ssem, rsem, lo=0, hi=row):
        @pl.loop(lo, hi)
        def _(i):
            for k in range(1, ny):
                to = lax.rem(y + k, ny) * row + lax.rem(t % row + i, row)
                rcopy(src.at[to], dst.at[t], ssem, rsem, d, to).start()

    def a2a_all(src, dst, ssem, rsem):
        return rcopy(
            src.at[pl.ds(0, nt - 1)], dst.at[pl.ds(0, nt - 1)], ssem, rsem, d, lax.rem(t + 1, nt)
        )

    def gu_out(h):
        return ws_gu.at[h], wr_gu[h], wgu_s.at[h], wgu_r.at[h]

    dn_out = (ws_dn, wr_dn, wdn_s, wdn_r)

    a2a_row(*gu_out(0))
    a2a_off(*gu_out(0))

    loads[4].wait()
    pick = onehot((rr, bs), lambda r, q: q == r + d * rr)
    en = 8 if ne % 8 == 0 else ne

    @pl.loop(0, ne // en)
    def _(i):
        blocks = dn_in[pl.ds(i * en, en)].reshape(en * bs, bs)
        res = lax.dot_general(pick, blocks, nt_dims, preferred_element_type=F32).astype(BF)
        for k in range(en):
            dn_t[i * en + k] = res[:, k * bs : (k + 1) * bs]

    @pl.loop(0, nt)
    def _(s):
        ws_dn[s] = dn_t[idx[stride + s]]

    wr_dn[t] = ws_dn[t]

    def row_of(yy):
        return pl.ds(yy * nz, nz)

    def yg(a, k, src):
        yy = lax.rem(y + k, ny)
        return rcopy(
            xall.at[a, row_of(y), :, my_half],
            xall.at[a, row_of(src), :, my_half],
            yg_s.at[a, k],
            yg_r.at[a, k],
            d,
            (yy * nz + z) * 2 + c,
        )

    def y_send(a):
        for i in range(nz):
            for k in range(1, ny):
                yy = lax.rem(y + k, ny)
                piece = xall.at[a, y * nz + i, :, my_half]
                rcopy(
                    piece, piece, yg_s.at[a, k], yg_r.at[a, k], d, (yy * nz + z) * 2 + c
                ).start()

    def to_core(a, k, lanes):
        yy = lax.rem(y - k + ny, ny)
        return rcopy(
            xall.at[a, row_of(yy), :, my_half],
            xall.at[a, row_of(yy), :, lanes],
            cg_s.at[a, k],
            cg_r.at[a, k],
            d,
            other,
        )

    def y_wait(a):
        for k in range(1, ny):
            yg(a, k, lax.rem(y - k + ny, ny)).wait_recv()
            to_core(a, k, my_half).start()

    def core_wait(a):
        for k in range(ny):
            to_core(a, k, its_half).wait_recv()

    x_wait(0)
    y_send(0)
    to_core(0, 0, my_half).start()
    x_out_all(1, lambda cp: cp.start())
    a2a_row(*gu_out(1))
    a2a_off(*gu_out(1))

    y_wait(0)
    x_wait(1)
    y_send(1)
    to_core(1, 0, my_half).start()
    a2a_row(*dn_out)
    a2a_off(*dn_out)
    core_wait(0)

    def partials(lo, arr, store):
        @pl.loop(0, own)
        def _(f):
            cols = pl.ds(pl.multiple_of(lo + f * bs, bs), bs)
            lhs = wd[:, :, cols].reshape(kall, bs)
            rhs = xall[arr].reshape(kall, tok)
            store(f, lax.dot_general(lhs, rhs, tn_dims, preferred_element_type=F32).astype(BF))

    def partials_gu(h):
        def store(f, res):
            part[h, pl.ds(pl.multiple_of(f * bs, bs), bs), :] = res

        partials((1 + h) * fown, 0, store)

    def store_hg(f, res):
        part_d[f] = res.reshape(2, hb, tok)

    def dp_gu(h, k):
        dd = lax.rem(d + k, nx)
        dst_tok = pl.ds(pl.multiple_of(dd * tk, tk), tk)
        return rcopy(
            part.at[h, :, dst_tok], psum_in.at[k, h], ph_s.at[h, k], ph_r.at[h, k], dd, t
        )

    def dp_dn(k):
        dd = lax.rem(d + k, nx)
        dst_tok = pl.ds(pl.multiple_of(dd * tk, tk), tk)
        return rcopy(part_d.at[:, :, :, dst_tok], psum_d.at[k], pd_s.at[k], pd_r.at[k], dd, t)

    def unpack_gu(h):
        @pl.loop(0, db)
        def _(a):
            for jl in range(own):
                s = idx[nt + jl * db + a]
                wd[a, :, pl.ds((1 + h) * fown + jl * bs, bs)] = wr_gu[h][s]

    for h in range(2):
        a2a_all(*gu_out(h)).wait_recv()
        unpack_gu(h)
        partials_gu(h)
        for k in range(1, nx):
            dp_gu(h, k).start()

    y_wait(1)

    def gu_total(h, j, lo):
        r = pl.ds(pl.multiple_of(j * bs + lo, hb), hb)
        acc = part[h, r, my_tok].astype(F32)
        for k in range(1, nx):
            acc += psum_in[k, h, r, :].astype(F32)
        return acc

    def gate_parts(h, j):
        gate = gu_total(h, j, 0)
        up = gu_total(h, j, hb)
        sig = 1.0 / (1.0 + jnp.exp(-gate))
        return gate, up, sig, gate * sig

    def h_gu(h, k, src):
        tok_src = pl.ds(pl.multiple_of(src * tk, tk), tk)
        dd = lax.rem(d + k, nx)
        return rcopy(
            hid_g.at[h, :, my_tok], hid_g.at[h, :, tok_src], hg_s.at[h, k], hg_r.at[h, k], dd, t
        )

    def h_dn(k, src):
        tok_src = pl.ds(pl.multiple_of(src * tk, tk), tk)
        dd = lax.rem(d + k, nx)
        return rcopy(
            hid_d.at[:, :, :, my_tok], hid_d.at[:, :, :, tok_src], hd_s.at[k], hd_r.at[k], dd, t
        )

    def from_plane(k):
        return lax.rem(d - k + nx, nx)

    for h in range(2):
        for k in range(1, nx):
            dp_gu(h, k).wait_recv()

        @pl.loop(0, own)
        def _(j):
            _, up, _, act = gate_parts(h, j)
            hid_d[j, h, :, my_tok] = (act * up).astype(BF)

    for k in range(1, nx):
        h_dn(k, d).start()

    core_wait(1)
    a2a_all(*dn_out).wait_recv()

    @pl.loop(0, db)
    def _(a):
        for jl in range(own):
            s = idx[stride + nt + jl * db + a]
            wd[a, :, pl.ds(jl * bs, bs)] = wr_dn[s]

    partials(0, 1, store_hg)
    for k in range(1, nx):
        dp_dn(k).start()

    mt = 256 // rr

    def grads(arr, rhs, store):
        @pl.loop(0, db // mt)
        def _(i):
            lhs = xall[arr, pl.ds(i * mt, mt)].reshape(mt * rr, tok)
            res = lax.dot_general(lhs, rhs(), nt_dims, preferred_element_type=F32).astype(BF)
            for jl in range(own):
                store(jl * db + i * mt, res[:, jl * bs : (jl + 1) * bs].reshape(mt, rr, bs))

    def grads_gu(h):
        def store(c0, v):
            gc[h, pl.ds(c0, mt)] = v

        grads(0, lambda: hid_g[h], store)

        @pl.loop(0, nt)
        def _(s):
            gs_gu[h, s] = gc[h, idx[nt + cells + s]]

        gr_gu[h][t] = gs_gu[h, t]

    def gu_back(h):
        return gs_gu.at[h], gr_gu[h], ggu_s.at[h], ggu_r.at[h]

    dn_back = (gs_dn, gr_dn, gdn_s, gdn_r)

    def store_dn(c0, v):
        gd[pl.ds(c0, mt)] = v

    for k in range(1, nx):
        h_dn(k, from_plane(k)).wait_recv()
    grads(1, lambda: hid_d[...].reshape(fown, tok), store_dn)

    @pl.loop(0, nt)
    def _(s):
        gs_dn[s] = gd[idx[stride + nt + cells + s]]

    gr_dn[t] = gs_dn[t]
    a2a_off(*dn_back)
    a2a_row(*dn_back)

    def core_out(a):
        return rcopy(oall.at[a, :, :, its_half], c_in.at[a], co_s.at[a], co_r.at[a], d, other)

    def in_half(a, p):
        return oall[a, p, :, my_half].astype(F32)

    def yo(a, k):
        yy = lax.rem(y + k, ny)
        return rcopy(
            tsum.at[a, row_of(yy)],
            y_in.at[a, k],
            yo_s.at[a, k],
            yo_r.at[a, k],
            d,
            (yy * nz + z) * 2 + c,
        )

    def sum_core(a):
        core_out(a).wait_recv()

        @pl.loop(0, npl)
        def _(p):
            tsum[a, p] = (in_half(a, p) + c_in[a, p].astype(F32)).astype(BF)

        for i in range(nz):
            for k in range(1, ny):
                yy = lax.rem(y + k, ny)
                rcopy(
                    tsum.at[a, yy * nz + i],
                    y_in.at[a, k, i],
                    yo_s.at[a, k],
                    yo_r.at[a, k],
                    d,
                    (yy * nz + z) * 2 + c,
                ).start()

    def fo(a, j, zz, go):
        core = d // dpc
        plane = c * dpc + j

        @pl.when(jnp.logical_not(self_piece(plane, zz, core)))
        def _():
            go(
                rcopy(
                    usum.at[a, zz, :, pl.ds(j * tk, tk)],
                    f_in.at[a, d % dpc, z],
                    fo_s.at[a, j, zz],
                    fo_r.at[a, d % dpc, z],
                    plane,
                    (y * nz + zz) * 2 + core,
                )
            )

    def fo_all(a, go):
        for k in range(nz):
            for j in range(dpc):
                fo(a, j, lax.rem(z + k, nz), go)

    def sum_y(a):
        for k in range(1, ny):
            yo(a, k).wait_recv()

        @pl.loop(0, nz)
        def _(p):
            acc = tsum[a, y * nz + p].astype(F32)
            for k in range(1, ny):
                acc += y_in[a, k, p].astype(F32)
            usum[a, p] = acc.astype(BF)

        fo_all(a, lambda cp: cp.start())

        @pl.when(d // dpc == c)
        def _():
            mine = pl.ds(pl.multiple_of(d % dpc * tk, tk), tk)
            f_in[a, d % dpc, z] = usum[a, z, :, mine]

    def sum_z(a, ref):
        for j in range(dpc):
            for zz in range(nz):

                @pl.when(jnp.logical_not(self_piece(c * dpc + j, zz, d // dpc)))
                def _():
                    rcopy(
                        xs.at[0, 0],
                        f_in.at[a, j, zz],
                        fo_s.at[0, 0, 0],
                        fo_r.at[a, j, zz],
                        d,
                        other,
                    ).wait_recv()

            acc = f_in[a, j, 0].astype(F32)
            for zz in range(1, nz):
                acc += f_in[a, j, zz].astype(F32)
            ref[j] = acc.astype(BF)

    def weights_times(a, lo, size, rhs):
        @pl.loop(0, db // mt)
        def _(i):
            arows = pl.ds(i * mt, mt)
            lhs = wd[arows, :, pl.ds(lo, size)].reshape(mt * rr, size)
            res = jnp.dot(lhs, rhs(), preferred_element_type=F32)
            oall[a, arows] = res.astype(BF).reshape(mt, rr, tok)

    weights_times(0, 0, fown, lambda: hid_d[...].reshape(fown, tok))
    core_out(0).start()

    for k in range(1, nx):
        dp_dn(k).wait_recv()
    for h in range(2):

        @pl.loop(0, own)
        def _(j):
            gate, up, sig, act = gate_parts(h, j)
            hg = part_d[j, h, :, my_tok].astype(F32)
            for k in range(1, nx):
                hg += psum_d[k, j, h].astype(F32)
            g0 = pl.multiple_of(j * bs, bs)
            hid_g[h, pl.ds(g0, hb), my_tok] = (
                hg * up * sig * (1.0 + gate * (1.0 - sig))
            ).astype(BF)
            hid_g[h, pl.ds(g0 + hb, hb), my_tok] = (hg * act).astype(BF)

        for k in range(1, nx):
            h_gu(h, k, d).start()

    sum_core(0)

    for h in range(2):
        for k in range(1, nx):
            h_gu(h, k, from_plane(k)).wait_recv()
        grads_gu(h)
        a2a_off(*gu_back(h))
        a2a_row(*gu_back(h))

    weights_times(1, fown, 2 * fown, lambda: hid_g[...].reshape(2 * fown, tok))
    core_out(1).start()

    sum_y(0)

    sum_core(1)

    a2a_all(*dn_back).wait_recv()
    groups = ne // nx

    @pl.loop(0, groups)
    def _(g):
        for p in range(nx):
            o = idx[stride + nt + cells + nt + g * nx + p]
            zl[g, :, pl.ds(p * bs, bs)] = gr_dn[o]

    for dd in range(nx):
        perm = onehot(
            (nx * bs, bs), lambda r, q: r == (q // rr) * bs + dd * rr + q % rr
        )
        moved = jnp.dot(zl[...].reshape(groups * rr, nx * bs), perm, preferred_element_type=F32)
        zs[dd] = moved.astype(BF).reshape(groups, rr, bs)
    zr[d] = zs[d]

    def zx(k, src):
        dd = lax.rem(d + k, nx)
        return rcopy(zs.at[dd], zr.at[src], zx_s.at[k], zx_r.at[k], dd, t)

    for i in range(groups):
        for k in range(1, nx):
            dd = lax.rem(d + k, nx)
            rcopy(zs.at[dd, i], zr.at[d, i], zx_s.at[k], zx_r.at[k], dd, t).start()

    sum_y(1)

    for k in range(1, nx):
        zx(k, from_plane(k)).wait_recv()
    eye_b = onehot((bs, bs), lambda r, q: r == q)

    @pl.loop(0, groups)
    def _(g):
        block = zr[:, g].reshape(nx * rr, bs)
        flip = lax.dot_general(block, eye_b, tn_dims, preferred_element_type=F32)
        dg_ref[pl.ds(g * nx, nx)] = flip.astype(BF).reshape(nx, rr, bs)

    a2a_all(*gu_back(0)).wait_recv()

    def unpack_half(h):
        @pl.loop(0, ne)
        def _(e):
            stage[e, :, pl.ds(h * bs, bs)] = gr_gu[h][idx[nt + cells + nt + e]]

    unpack_half(0)

    sum_z(0, out_ref)
    sum_z(1, in_ref)

    a2a_all(*gu_back(1)).wait_recv()
    unpack_half(1)

    @pl.loop(0, ne // me_n)
    def _(i):
        es = pl.ds(i * me_n, me_n)
        both = stage[es].reshape(me_n * rr, 2 * bs)
        res = jnp.dot(both, halves, preferred_element_type=F32).astype(BF)
        gg_ref[es] = res[:, :bs].reshape(me_n, rr, bs)
        ug_ref[es] = res[:, bs:].reshape(me_n, rr, bs)

    for a in range(2):
        x_out_all(a, lambda cp: cp.wait_send())
        fo_all(a, lambda cp: cp.wait_send())
        core_out(a).wait_send()
        for k in range(1, ny):
            yg(a, k, y).wait_send()
            yo(a, k).wait_send()
        for k in range(ny):
            to_core(a, k, my_half).wait_send()
    for h in range(2):
        a2a_all(*gu_out(h)).wait_send()
        a2a_all(*gu_back(h)).wait_send()
    a2a_all(*dn_out).wait_send()
    a2a_all(*dn_back).wait_send()
    for k in range(1, nx):
        for h in range(2):
            dp_gu(h, k).wait_send()
            h_gu(h, k, d).wait_send()
        dp_dn(k).wait_send()
        h_dn(k, d).wait_send()
        zx(k, d).wait_send()


def copy_kernel(n, *refs):
    for i in range(n):
        refs[n + i][...] = refs[i][...]


def per_device(dims, tokens_in, out_grad, gate_blocks, up_blocks, down_blocks, gate_up_index, down_index):
    nx, ny, nz = dims
    nt, ne = gate_up_index.shape[:2]
    npl = ny * nz
    db = npl
    bs = gate_blocks.shape[1]
    tk = tokens_in.shape[0]
    own = FB // nt
    rr = bs // nx
    dpc = nx // 2
    fown = own * bs
    tok = nx * tk
    cells = own * db
    tables = route_tables(
        (
            (gate_up_index[:, :, 1], gate_up_index[:, :, 0]),
            (down_index[:, :, 0], down_index[:, :, 1]),
        ),
        own,
        db,
        lax.axis_index("tensor"),
    )
    v = lambda *s: pltpu.VMEM(s, BF)
    dma = lambda *s: pltpu.SemaphoreType.DMA(s)
    scratch = [
        v(2, ne, rr, bs),
        v(2, ne + 1, rr, bs),
        v(ne, bs, bs),
        v(ne + 1, rr, bs),
        v(2, dpc, rr, tk),
        v(2, nt, rr, bs),
        v(nt + 1, rr, bs),
        v(nt + 1, rr, bs),
        v(nt, rr, bs),
        v(nt + 1, rr, bs),
        v(2, npl, rr, tok),
        v(db, rr, 3 * fown),
        v(2, fown, tok),
        v(nx, 2, fown, tk),
        v(own, 2, bs // 2, tok),
        v(nx, own, 2, bs // 2, tk),
        v(2, fown, tok),
        v(own, 2, bs // 2, tok),
        v(2, npl, rr, tok),
        v(2, npl, rr, tok // 2),
        v(2, npl, rr, tok // 2),
        v(2, ny, nz, rr, tok // 2),
        v(2, nz, rr, tok // 2),
        v(2, dpc, nz, rr, tk),
        v(2, cells, rr, bs),
        v(cells, rr, bs),
        v(2, nt, rr, bs),
        v(nt, rr, bs),
        v(nt, rr, bs),
        v(nt, rr, bs),
        v(nt, rr, bs),
        v(ne, rr, 2 * bs),
        v(ne // nx, rr, nx * bs),
        v(nx, ne // nx, rr, bs),
        v(nx, ne // nx, rr, bs),
        dma(5),
        dma(2, dpc, nz),
        dma(2, nz, dpc),
        dma(2, ny),
        dma(2, ny),
        dma(2, ny),
        dma(2, ny),
        pltpu.SemaphoreType.DMA,
        pltpu.SemaphoreType.DMA,
        dma(2),
        dma(2),
        dma(2, nx),
        dma(2, nx),
        dma(nx),
        dma(nx),
        dma(2, nx),
        dma(2, nx),
        dma(nx),
        dma(nx),
        dma(2),
        dma(2),
        dma(2, ny),
        dma(2, ny),
        dma(2, dpc, nz),
        dma(2, dpc, nz),
        pltpu.SemaphoreType.DMA,
        pltpu.SemaphoreType.DMA,
        dma(2),
        dma(2),
        dma(nx),
        dma(nx),
    ]
    vm = pl.BlockSpec(memory_space=pltpu.VMEM)
    hbm = pl.BlockSpec(memory_space=pl.ANY)
    grad = jax.ShapeDtypeStruct((ne, rr, bs), BF)
    act = jax.ShapeDtypeStruct((dpc, rr, tk), BF)
    feat = dpc * rr
    shapes = (act, act, grad, grad, grad)
    results = pl.pallas_call(
        functools.partial(kernel, (nx, ny, nz, ne, own, db)),
        out_shape=shapes,
        in_specs=[pl.BlockSpec(memory_space=pltpu.SMEM)] + [hbm] * 5,
        out_specs=(vm,) * 5,
        scratch_shapes=scratch,
        compiler_params=pltpu.CompilerParams(
            collective_id=0, has_side_effects=True, vmem_limit_bytes=56 * 2**20
        ),
    )(
        tables,
        tokens_in.T.reshape(dpc, rr, tk),
        out_grad.T.reshape(dpc, rr, tk),
        gate_blocks,
        up_blocks,
        down_blocks,
    )
    n = len(shapes)
    results = pl.pallas_call(
        functools.partial(copy_kernel, n),
        out_shape=shapes,
        in_specs=[vm] * n,
        out_specs=(vm,) * n,
    )(*results)
    return tuple(r.reshape(feat, tk).T for r in results[:2]) + tuple(results[2:])


FB = 128
GRID = {4: (4, 8)}


def solution(mesh):
    nx, nt = mesh.shape["dp"], mesh.shape["tensor"]
    ny, nz = GRID[nx]
    in_specs = (
        P("dp", "tensor"),
        P("dp", "tensor"),
        P("tensor", None, None),
        P("tensor", None, None),
        P("tensor", None, None),
        P(),
        P(),
    )
    out_specs = (
        P("dp", "tensor"),
        P("dp", "tensor"),
        P("tensor", "dp", None),
        P("tensor", "dp", None),
        P("tensor", "dp", None),
    )
    return jax.shard_map(
        functools.partial(per_device, (nx, ny, nz)),
        mesh=mesh,
        in_specs=in_specs,
        out_specs=out_specs,
        check_vma=False,
    )
```

time: 127 us -> 112 us (0.88)
  Pallas kernels: 124 us -> 109 us
    pallas_call x1, Pallas kernels: 122 us -> 107 us  [per_device(): pl.pallas_call(functools.partial(kernel, (nx, ny, nz, ne, own, db)), out_...]
where the time goes in v3:
time: 112 us
  Pallas kernels  109 us (97%)
  local copies, waits for them, and re-layouts  1.75 us (2%)
    pallas_call x1, Pallas kernels, per_device(): pl.pallas_call(functools.partial(kernel, (nx, ny, nz, ne, own, db)), out_...  107 us

profile of v3, /device:TPU:1, one launch (start us, length us, event | category | flops | bytes accessed | tf_op | source)
XLA Modules:
  0.0 111.6 jit_solution(17004534107804426884)
XLA Ops:
  0.6 0.0 copy-start
  0.6 0.9 fusion.5
  1.5 0.0 copy-done
  1.6 0.1 fusion.3
  1.6 0.2 dynamic-slice_reduce_fusion
  1.8 0.1 select_reduce_fusion.1
  1.9 0.1 select_reduce_fusion
  2.0 0.1 pad_add_fusion.1
  2.1 0.7 reshape.26.idx
  2.8 106.7 %shard_map.110 = (bf16[2,32,128]{2,1,0:T(8,128)(2,1)}, bf16[2,32,128]{2,1,0:T(8,128)(2,1)}, bf16[32,32,128]{2,1,0:T(8,128)(2,1)}, bf16[32,32,128]{2,1,0:T(8,128)(2,1)}, bf16[32,32,128]{2,1,0:T(8,128)(2,1)}) custom-call(s32[448]{0:T(512)} %reshape.26.idx, bf16[2,32,128]{2,1,0:T(8,128)(2,1)} %bitcast.26, bf16[2,32,128]{2,1,0:T(8,128)(2,1)} %bitcast.27, ...), custom_call_target="tpu_custom_call" | custom-call | tf_op jit(solution)/shard_map/pallas_call | solution.py:845
  109.5 2.0 %shard_map.111 = (bf16[2,32,128]{2,1,0:T(8,128)(2,1)}, bf16[2,32,128]{2,1,0:T(8,128)(2,1)}, bf16[32,32,128]{2,1,0:T(8,128)(2,1)}, bf16[32,32,128]{2,1,0:T(8,128)(2,1)}, bf16[32,32,128]{2,1,0:T(8,128)(2,1)}) custom-call(bf16[2,32,128]{2,1,0:T(8,128)(2,1)} %get-tuple-element.15.refs_0_, bf16[2,32,128]{2,1,0:T(8,128)(2,1)} %get-tuple-element.16.refs_1_, ...), custom_call_target="tpu_custom_call" | custom-call | tf_op jit(solution)/shard_map/pallas_call | solution.py:863
  (2 shorter events, 0.0 us)
Async XLA Ops:
  0.6 0.9 copy-start

commit v4 on v3

--- a/solution.py
+++ b/solution.py
@@ -42,7 +42,6 @@
     ug_ref,
     dg_ref,
     gu_in,
-    gu_ab,
     dn_in,
     dn_t,
     xs,
@@ -72,7 +71,6 @@
     gr_b,
     gs_dn,
     gr_dn,
-    stage,
     zl,
     zs,
     zr,
@@ -153,8 +151,8 @@
 
     rows = pl.ds(pl.multiple_of(d * rr, rr), rr)
     loads = [
-        pltpu.make_async_copy(gate_hbm.at[:, rows, :], gu_in.at[0], load_sem.at[0]),
-        pltpu.make_async_copy(up_hbm.at[:, rows, :], gu_in.at[1], load_sem.at[1]),
+        pltpu.make_async_copy(gate_hbm.at[:, rows, :], gu_in.at[0, pl.ds(0, ne)], load_sem.at[0]),
+        pltpu.make_async_copy(up_hbm.at[:, rows, :], gu_in.at[1, pl.ds(0, ne)], load_sem.at[1]),
         pltpu.make_async_copy(x_hbm, xs.at[0], load_sem.at[2]),
         pltpu.make_async_copy(dy_hbm, xs.at[1], load_sem.at[3]),
         pltpu.make_async_copy(down_hbm, dn_in, load_sem.at[4]),
@@ -178,6 +176,24 @@
                 device_id=(lax.rem(d + k, nx), y * nz * 2 + i),
                 device_id_type=MESH,
             )
+
+    zero_rows = jnp.zeros((rr, bs), BF)
+    dn_t[ne] = zero_rows
+    wr_dn[nt] = zero_rows
+    for h in range(2):
+        gu_in[h, ne] = zero_rows
+        wr_gu[h][nt] = zero_rows
+    loads[0].wait()
+    loads[1].wait()
+
+    @pl.loop(0, nt)
+    def _(s):
+        e = idx[s]
+        ws_gu[0, s] = gu_in[0, e]
+        ws_gu[1, s] = gu_in[1, e]
+
+    for h in range(2):
+        wr_gu[h][t] = ws_gu[h, t]
 
     loads[2].wait()
     loads[3].wait()
@@ -234,40 +250,6 @@
         for a in range(2):
             xall[a, chip, :, my_tok] = xs[a, d % dpc]
 
-    zero_rows = jnp.zeros((rr, bs), BF)
-    dn_t[ne] = zero_rows
-    wr_dn[nt] = zero_rows
-    for h in range(2):
-        gu_ab[h, ne] = zero_rows
-        wr_gu[h][nt] = zero_rows
-
-    def half_src(i):
-        return (i % bs) // hb * bs + i // bs * hb + i % hb
-
-    halves = onehot((2 * bs, 2 * bs), lambda r, q: r == half_src(q))
-    loads[0].wait()
-    loads[1].wait()
-    me_n = 256 // rr
-
-    @pl.loop(0, ne // me_n)
-    def _(i):
-        es = pl.ds(i * me_n, me_n)
-        both = jnp.concatenate(
-            [gu_in[0, es].reshape(me_n * rr, bs), gu_in[1, es].reshape(me_n * rr, bs)], axis=1
-        )
-        res = jnp.dot(both, halves, preferred_element_type=F32).astype(BF)
-        for h in range(2):
-            gu_ab[h, es] = res[:, h * bs : (h + 1) * bs].reshape(me_n, rr, bs)
-
-    @pl.loop(0, nt)
-    def _(s):
-        e = idx[s]
-        ws_gu[0, s] = gu_ab[0, e]
-        ws_gu[1, s] = gu_ab[1, e]
-
-    for h in range(2):
-        wr_gu[h][t] = ws_gu[h, t]
-
     row = 2 * nz
 
     def a2a_row(src, dst, ssem, rsem):
@@ -386,7 +368,7 @@
         partials((1 + h) * fown, 0, store)
 
     def store_hg(f, res):
-        part_d[f] = res.reshape(2, hb, tok)
+        part_d[pl.ds(pl.multiple_of(f * bs, bs), bs), :] = res
 
     def dp_gu(h, k):
         dd = lax.rem(d + k, nx)
@@ -398,7 +380,7 @@
     def dp_dn(k):
         dd = lax.rem(d + k, nx)
         dst_tok = pl.ds(pl.multiple_of(dd * tk, tk), tk)
-        return rcopy(part_d.at[:, :, :, dst_tok], psum_d.at[k], pd_s.at[k], pd_r.at[k], dd, t)
+        return rcopy(part_d.at[:, dst_tok], psum_d.at[k], pd_s.at[k], pd_r.at[k], dd, t)
 
     def unpack_gu(h):
         @pl.loop(0, db)
@@ -416,18 +398,23 @@
 
     y_wait(1)
 
-    def gu_total(h, j, lo):
-        r = pl.ds(pl.multiple_of(j * bs + lo, hb), hb)
-        acc = part[h, r, my_tok].astype(F32)
+    def plane_sum(mine, theirs):
+        acc = mine.astype(F32)
         for k in range(1, nx):
-            acc += psum_in[k, h, r, :].astype(F32)
+            acc += theirs(k).astype(F32)
         return acc
 
-    def gate_parts(h, j):
-        gate = gu_total(h, j, 0)
-        up = gu_total(h, j, hb)
+    def gate_parts(r):
+        gate, up = (
+            plane_sum(part[h, r, my_tok], lambda k, h=h: psum_in[k, h, r, :]) for h in range(2)
+        )
         sig = 1.0 / (1.0 + jnp.exp(-gate))
         return gate, up, sig, gate * sig
+
+    def each_rows(fn):
+        @pl.loop(0, fown // hb)
+        def _(j):
+            fn(pl.ds(pl.multiple_of(j * hb, hb), hb))
 
     def h_gu(h, k, src):
         tok_src = pl.ds(pl.multiple_of(src * tk, tk), tk)
@@ -440,7 +427,7 @@
         tok_src = pl.ds(pl.multiple_of(src * tk, tk), tk)
         dd = lax.rem(d + k, nx)
         return rcopy(
-            hid_d.at[:, :, :, my_tok], hid_d.at[:, :, :, tok_src], hd_s.at[k], hd_r.at[k], dd, t
+            hid_d.at[:, my_tok], hid_d.at[:, tok_src], hd_s.at[k], hd_r.at[k], dd, t
         )
 
     def from_plane(k):
@@ -450,11 +437,11 @@
         for k in range(1, nx):
             dp_gu(h, k).wait_recv()
 
-        @pl.loop(0, own)
-        def _(j):
-            _, up, _, act = gate_parts(h, j)
-            hid_d[j, h, :, my_tok] = (act * up).astype(BF)
-
+    def hidden_rows(r):
+        _, up, _, act = gate_parts(r)
+        hid_d[r, my_tok] = (act * up).astype(BF)
+
+    each_rows(hidden_rows)
     for k in range(1, nx):
         h_dn(k, d).start()
 
@@ -503,7 +490,7 @@
 
     for k in range(1, nx):
         h_dn(k, from_plane(k)).wait_recv()
-    grads(1, lambda: hid_d[...].reshape(fown, tok), store_dn)
+    grads(1, lambda: hid_d[...], store_dn)
 
     @pl.loop(0, nt)
     def _(s):
@@ -617,43 +604,44 @@
             res = jnp.dot(lhs, rhs(), preferred_element_type=F32)
             oall[a, arows] = res.astype(BF).reshape(mt, rr, tok)
 
-    weights_times(0, 0, fown, lambda: hid_d[...].reshape(fown, tok))
+    weights_times(0, 0, fown, lambda: hid_d[...])
     core_out(0).start()
 
     for k in range(1, nx):
         dp_dn(k).wait_recv()
+
+    def grad_rows(r):
+        gate, up, sig, act = gate_parts(r)
+        hg = plane_sum(part_d[r, my_tok], lambda k: psum_d[k, r, :])
+        hid_g[0, r, my_tok] = (hg * up * sig * (1.0 + gate * (1.0 - sig))).astype(BF)
+        hid_g[1, r, my_tok] = (hg * act).astype(BF)
+
+    each_rows(grad_rows)
     for h in range(2):
-
-        @pl.loop(0, own)
-        def _(j):
-            gate, up, sig, act = gate_parts(h, j)
-            hg = part_d[j, h, :, my_tok].astype(F32)
-            for k in range(1, nx):
-                hg += psum_d[k, j, h].astype(F32)
-            g0 = pl.multiple_of(j * bs, bs)
-            hid_g[h, pl.ds(g0, hb), my_tok] = (
-                hg * up * sig * (1.0 + gate * (1.0 - sig))
-            ).astype(BF)
-            hid_g[h, pl.ds(g0 + hb, hb), my_tok] = (hg * act).astype(BF)
-
         for k in range(1, nx):
             h_gu(h, k, d).start()
 
     sum_core(0)
 
-    for h in range(2):
+    def h_wait(h):
         for k in range(1, nx):
             h_gu(h, k, from_plane(k)).wait_recv()
-        grads_gu(h)
-        a2a_off(*gu_back(h))
-        a2a_row(*gu_back(h))
+
+    h_wait(0)
+    grads_gu(0)
+    a2a_off(*gu_back(0))
+    a2a_row(*gu_back(0))
+    h_wait(1)
 
     weights_times(1, fown, 2 * fown, lambda: hid_g[...].reshape(2 * fown, tok))
     core_out(1).start()
+    grads_gu(1)
+
+    sum_core(1)
+    a2a_off(*gu_back(1))
+    a2a_row(*gu_back(1))
 
     sum_y(0)
-
-    sum_core(1)
 
     a2a_all(*dn_back).wait_recv()
     groups = ne // nx
@@ -693,28 +681,19 @@
         flip = lax.dot_general(block, eye_b, tn_dims, preferred_element_type=F32)
         dg_ref[pl.ds(g * nx, nx)] = flip.astype(BF).reshape(nx, rr, bs)
 
-    a2a_all(*gu_back(0)).wait_recv()
-
-    def unpack_half(h):
+    def unpack(h, ref):
+        a2a_all(*gu_back(h)).wait_recv()
+
         @pl.loop(0, ne)
         def _(e):
-            stage[e, :, pl.ds(h * bs, bs)] = gr_gu[h][idx[nt + cells + nt + e]]
-
-    unpack_half(0)
+            ref[e] = gr_gu[h][idx[nt + cells + nt + e]]
+
+    unpack(0, gg_ref)
 
     sum_z(0, out_ref)
     sum_z(1, in_ref)
 
-    a2a_all(*gu_back(1)).wait_recv()
-    unpack_half(1)
-
-    @pl.loop(0, ne // me_n)
-    def _(i):
-        es = pl.ds(i * me_n, me_n)
-        both = stage[es].reshape(me_n * rr, 2 * bs)
-        res = jnp.dot(both, halves, preferred_element_type=F32).astype(BF)
-        gg_ref[es] = res[:, :bs].reshape(me_n, rr, bs)
-        ug_ref[es] = res[:, bs:].reshape(me_n, rr, bs)
+    unpack(1, ug_ref)
 
     for a in range(2):
         x_out_all(a, lambda cp: cp.wait_send())
@@ -740,8 +719,12 @@
 
 
 def copy_kernel(n, *refs):
-    for i in range(n):
-        refs[n + i][...] = refs[i][...]
+    sem = refs[-1]
+    copies = [pltpu.make_async_copy(refs[i], refs[n + i], sem.at[i]) for i in range(n)]
+    for cp in copies:
+        cp.start()
+    for cp in copies:
+        cp.wait()
 
 
 def per_device(dims, tokens_in, out_grad, gate_blocks, up_blocks, down_blocks, gate_up_index, down_index):
@@ -769,7 +752,6 @@
     v = lambda *s: pltpu.VMEM(s, BF)
     dma = lambda *s: pltpu.SemaphoreType.DMA(s)
     scratch = [
-        v(2, ne, rr, bs),
         v(2, ne + 1, rr, bs),
         v(ne, bs, bs),
         v(ne + 1, rr, bs),
@@ -783,10 +765,10 @@
         v(db, rr, 3 * fown),
         v(2, fown, tok),
         v(nx, 2, fown, tk),
-        v(own, 2, bs // 2, tok),
-        v(nx, own, 2, bs // 2, tk),
+        v(fown, tok),
+        v(nx, fown, tk),
         v(2, fown, tok),
-        v(own, 2, bs // 2, tok),
+        v(fown, tok),
         v(2, npl, rr, tok),
         v(2, npl, rr, tok // 2),
         v(2, npl, rr, tok // 2),
@@ -800,7 +782,6 @@
         v(nt, rr, bs),
         v(nt, rr, bs),
         v(nt, rr, bs),
-        v(ne, rr, 2 * bs),
         v(ne // nx, rr, nx * bs),
         v(nx, ne // nx, rr, bs),
         v(nx, ne // nx, rr, bs),
@@ -864,7 +845,8 @@
         functools.partial(copy_kernel, n),
         out_shape=shapes,
         in_specs=[vm] * n,
-        out_specs=(vm,) * n,
+        out_specs=(hbm,) * n,
+        scratch_shapes=[pltpu.SemaphoreType.DMA((n,))],
     )(*results)
     return tuple(r.reshape(feat, tk).T for r in results[:2]) + tuple(results[2:])
 

time: 112 us -> 111 us (level)
  no operation moved by 1% of the time
where the time goes in v4:
time: 111 us
  Pallas kernels  108 us (97%)
  local copies, waits for them, and re-layouts  1.75 us (2%)
    pallas_call x1, Pallas kernels, per_device(): pl.pallas_call(functools.partial(kernel, (nx, ny, nz, ne, own, db)), out_...  106 us

profile of v4, /device:TPU:1, one launch (start us, length us, event | category | flops | bytes accessed | tf_op | source)
XLA Modules:
  0.0 111.2 jit_solution(14873514915492716880)
XLA Ops:
  0.6 0.0 copy-start
  0.6 0.9 fusion.5
  1.5 0.0 copy-done
  1.6 0.1 fusion.3
  1.6 0.2 dynamic-slice_reduce_fusion
  1.8 0.1 select_reduce_fusion.1
  1.9 0.1 select_reduce_fusion
  2.0 0.1 pad_add_fusion.1
  2.1 0.7 reshape.26.idx
  2.8 106.3 %shard_map.110 = (bf16[2,32,128]{2,1,0:T(8,128)(2,1)}, bf16[2,32,128]{2,1,0:T(8,128)(2,1)}, bf16[32,32,128]{2,1,0:T(8,128)(2,1)}, bf16[32,32,128]{2,1,0:T(8,128)(2,1)}, bf16[32,32,128]{2,1,0:T(8,128)(2,1)}) custom-call(s32[448]{0:T(512)} %reshape.26.idx, bf16[2,32,128]{2,1,0:T(8,128)(2,1)} %bitcast.26, bf16[2,32,128]{2,1,0:T(8,128)(2,1)} %bitcast.27, ...), custom_call_target="tpu_custom_call" | custom-call | tf_op jit(solution)/shard_map/pallas_call | solution.py:826
  109.1 2.1 %shard_map.111 = (bf16[2,32,128]{2,1,0:T(8,128)(2,1)}, bf16[2,32,128]{2,1,0:T(8,128)(2,1)}, bf16[32,32,128]{2,1,0:T(8,128)(2,1)}, bf16[32,32,128]{2,1,0:T(8,128)(2,1)}, bf16[32,32,128]{2,1,0:T(8,128)(2,1)}) custom-call(bf16[2,32,128]{2,1,0:T(8,128)(2,1)} %get-tuple-element.15.refs_0_, bf16[2,32,128]{2,1,0:T(8,128)(2,1)} %get-tuple-element.16.refs_1_, ...), custom_call_target="tpu_custom_call" | custom-call | tf_op jit(solution)/shard_map/pallas_call | solution.py:844
  (2 shorter events, 0.0 us)
Async XLA Ops:
  0.6 0.9 copy-start

commit v5 on v4

--- a/solution.py
+++ b/solution.py
@@ -160,22 +160,31 @@
     for cp in loads:
         cp.start()
 
-    @pl.loop(1, nt)
+    @pl.loop(0, 2 * nz)
     def _(i):
-        pl.semaphore_signal(
-            barrier, inc=1, device_id=(d, lax.rem(t + i, nt)), device_id_type=MESH
-        )
-
-    for k in range(1, nx):
-
-        @pl.loop(0, 2 * nz)
-        def _(i):
+        for k in range(1, nx):
             pl.semaphore_signal(
                 barrier,
                 inc=1,
                 device_id=(lax.rem(d + k, nx), y * nz * 2 + i),
                 device_id_type=MESH,
             )
+        for k in range(1, ny):
+            pl.semaphore_signal(
+                barrier,
+                inc=1,
+                device_id=(d, lax.rem(y + k, ny) * nz * 2 + i),
+                device_id_type=MESH,
+            )
+
+    @pl.loop(1, 2 * nz)
+    def _(i):
+        pl.semaphore_signal(
+            barrier,
+            inc=1,
+            device_id=(d, y * nz * 2 + lax.rem(t % (2 * nz) + i, 2 * nz)),
+            device_id_type=MESH,
+        )
 
     zero_rows = jnp.zeros((rr, bs), BF)
     dn_t[ne] = zero_rows
@@ -275,8 +284,8 @@
 
     dn_out = (ws_dn, wr_dn, wdn_s, wdn_r)
 
+    a2a_off(*gu_out(0))
     a2a_row(*gu_out(0))
-    a2a_off(*gu_out(0))
 
     loads[4].wait()
     pick = onehot((rr, bs), lambda r, q: q == r + d * rr)
@@ -342,8 +351,8 @@
     y_send(0)
     to_core(0, 0, my_half).start()
     x_out_all(1, lambda cp: cp.start())
+    a2a_off(*gu_out(1))
     a2a_row(*gu_out(1))
-    a2a_off(*gu_out(1))
 
     y_wait(0)
     x_wait(1)
@@ -639,7 +648,6 @@
 
     sum_core(1)
     a2a_off(*gu_back(1))
-    a2a_row(*gu_back(1))
 
     sum_y(0)
 
@@ -670,6 +678,7 @@
             rcopy(zs.at[dd, i], zr.at[d, i], zx_s.at[k], zx_r.at[k], dd, t).start()
 
     sum_y(1)
+    a2a_row(*gu_back(1))
 
     for k in range(1, nx):
         zx(k, from_plane(k)).wait_recv()

time: 111 us -> 110 us (level)
    pallas_call x1, Pallas kernels: 106 us -> 105 us  [per_device(): pl.pallas_call(functools.partial(kernel, (nx, ny, nz, ne, own, db)), out_...]
where the time goes in v5:
time: 110 us
  Pallas kernels  107 us (97%)
  local copies, waits for them, and re-layouts  1.75 us (2%)
    pallas_call x1, Pallas kernels, per_device(): pl.pallas_call(functools.partial(kernel, (nx, ny, nz, ne, own, db)), out_...  105 us

profile of v5, /device:TPU:1, one launch (start us, length us, event | category | flops | bytes accessed | tf_op | source)
XLA Modules:
  0.0 110.0 jit_solution(17716817926009702660)
XLA Ops:
  0.6 0.0 copy-start
  0.6 0.9 fusion.5
  1.5 0.0 copy-done
  1.6 0.1 fusion.3
  1.6 0.2 dynamic-slice_reduce_fusion
  1.8 0.1 select_reduce_fusion.1
  1.9 0.1 select_reduce_fusion
  2.0 0.1 pad_add_fusion.1
  2.1 0.7 reshape.26.idx
  2.8 105.2 %shard_map.110 = (bf16[2,32,128]{2,1,0:T(8,128)(2,1)}, bf16[2,32,128]{2,1,0:T(8,128)(2,1)}, bf16[32,32,128]{2,1,0:T(8,128)(2,1)}, bf16[32,32,128]{2,1,0:T(8,128)(2,1)}, bf16[32,32,128]{2,1,0:T(8,128)(2,1)}) custom-call(s32[448]{0:T(512)} %reshape.26.idx, bf16[2,32,128]{2,1,0:T(8,128)(2,1)} %bitcast.26, bf16[2,32,128]{2,1,0:T(8,128)(2,1)} %bitcast.27, ...), custom_call_target="tpu_custom_call" | custom-call | tf_op jit(solution)/shard_map/pallas_call | solution.py:835
  108.0 2.1 %shard_map.111 = (bf16[2,32,128]{2,1,0:T(8,128)(2,1)}, bf16[2,32,128]{2,1,0:T(8,128)(2,1)}, bf16[32,32,128]{2,1,0:T(8,128)(2,1)}, bf16[32,32,128]{2,1,0:T(8,128)(2,1)}, bf16[32,32,128]{2,1,0:T(8,128)(2,1)}) custom-call(bf16[2,32,128]{2,1,0:T(8,128)(2,1)} %get-tuple-element.15.refs_0_, bf16[2,32,128]{2,1,0:T(8,128)(2,1)} %get-tuple-element.16.refs_1_, ...), custom_call_target="tpu_custom_call" | custom-call | tf_op jit(solution)/shard_map/pallas_call | solution.py:853
  (2 shorter events, 0.0 us)
Async XLA Ops:
  0.6 0.9 copy-start

commit v6 on v5

--- a/solution.py
+++ b/solution.py
@@ -358,8 +358,8 @@
     x_wait(1)
     y_send(1)
     to_core(1, 0, my_half).start()
+    a2a_off(*dn_out)
     a2a_row(*dn_out)
-    a2a_off(*dn_out)
     core_wait(0)
 
     def partials(lo, arr, store):

time: 110 us -> 109 us (level)
    pallas_call x1, Pallas kernels: 105 us -> 104 us  [per_device(): pl.pallas_call(functools.partial(kernel, (nx, ny, nz, ne, own, db)), out_...]
where the time goes in v6:
time: 109 us; the launch traced here: 108 us
  Pallas kernels  106 us (97%)
  local copies, waits for them, and re-layouts  1.75 us (2%)
    pallas_call x1, Pallas kernels, per_device(): pl.pallas_call(functools.partial(kernel, (nx, ny, nz, ne, own, db)), out_...  104 us

profile of v6, /device:TPU:1, one launch (start us, length us, event | category | flops | bytes accessed | tf_op | source)
XLA Modules:
  0.0 108.4 jit_solution(17125333983392896989)
XLA Ops:
  0.6 0.0 copy-start
  0.6 0.9 fusion.5
  1.5 0.0 copy-done
  1.6 0.1 fusion.3
  1.6 0.2 dynamic-slice_reduce_fusion
  1.8 0.1 select_reduce_fusion.1
  1.9 0.1 select_reduce_fusion
  2.0 0.1 pad_add_fusion.1
  2.1 0.7 reshape.26.idx
  2.8 103.6 %shard_map.110 = (bf16[2,32,128]{2,1,0:T(8,128)(2,1)}, bf16[2,32,128]{2,1,0:T(8,128)(2,1)}, bf16[32,32,128]{2,1,0:T(8,128)(2,1)}, bf16[32,32,128]{2,1,0:T(8,128)(2,1)}, bf16[32,32,128]{2,1,0:T(8,128)(2,1)}) custom-call(s32[448]{0:T(512)} %reshape.26.idx, bf16[2,32,128]{2,1,0:T(8,128)(2,1)} %bitcast.26, bf16[2,32,128]{2,1,0:T(8,128)(2,1)} %bitcast.27, ...), custom_call_target="tpu_custom_call" | custom-call | tf_op jit(solution)/shard_map/pallas_call | solution.py:835
  106.4 2.1 %shard_map.111 = (bf16[2,32,128]{2,1,0:T(8,128)(2,1)}, bf16[2,32,128]{2,1,0:T(8,128)(2,1)}, bf16[32,32,128]{2,1,0:T(8,128)(2,1)}, bf16[32,32,128]{2,1,0:T(8,128)(2,1)}, bf16[32,32,128]{2,1,0:T(8,128)(2,1)}) custom-call(bf16[2,32,128]{2,1,0:T(8,128)(2,1)} %get-tuple-element.15.refs_0_, bf16[2,32,128]{2,1,0:T(8,128)(2,1)} %get-tuple-element.16.refs_1_, ...), custom_call_target="tpu_custom_call" | custom-call | tf_op jit(solution)/shard_map/pallas_call | solution.py:853
  (2 shorter events, 0.0 us)
Async XLA Ops:
  0.6 0.9 copy-start
